TPU v7x, 1024 devices: a whole 4x8x16 slice. The times are simulated.
1024 devices in a mesh: face: 16 (over z), blk: 64 (over y, x, core).
Axes of the slice: x: 4, y: 8, z: 16, core: 2. Of those that a mesh axis runs over, the one named last changes fastest.
Arguments:
- air_state: float32 [3, 16, 256, 8192], P(None, None, 'face', 'blk'), may hold values from -6 to 6
- air_wind: float32 [2, 16, 256, 8192], P(None, None, 'face', 'blk'), may hold values from -4 to 4
- jacobian: float32 [256, 8192], P('face', 'blk'), may hold values from 0.5 to 2
- land_area: float32 [256, 8192], P('face', 'blk'), may hold values from 0.1 to 1
- xgrid_rows: int32 [1024, 64, 128], P(('face', 'blk')), may hold values from 0 to 2047
- tracers: float32 [2, 16, 2097152], P(None, None, ('face', 'blk')), may hold values from -6 to 6
- edge_coef: float32 [6, 2097152], P(None, ('face', 'blk')), may hold values from 0.02 to 0.14
- neighbours: int32 [6, 2097152], P(None, ('face', 'blk')), may hold values from 0 to 2303
- vert_rate: float32 [2097152], P(('face', 'blk')), may hold values from 0.05 to 0.2
- ocean_area: float32 [2097152], P(('face', 'blk')), may hold values from 0.5 to 2
- send_list: int32 [1024, 256], P(('face', 'blk')), may hold values from 0 to 2047
- xgrid_cols: int32 [1024, 64, 128], P(('face', 'blk')), may hold values from 0 to 2047
- xgrid_weights: float32 [1024, 64, 128], P(('face', 'blk')), may hold values from 0 to 1, as said below
Outputs:
- air_final: float32 [3, 16, 256, 8192], P(None, None, 'face', 'blk')
- ocean_final: float32 [2, 16, 2097152], P(None, None, ('face', 'blk'))
Inputs may be any that keep to these rules, and one draw needn't show every extreme that they name: `xgrid_weights`: in every block of 128 slots the nonzero weights, each at least 0.1, come first and zeros fill the rest; in every draw some blocks of every device are completely full.
All inputs are finite; a program needn't handle non-finite values.
Results may differ from a plain program's by a relative error of at most 0.00016.
Values sent between devices are 32-bit elements; how exact they have to be, the bound alone decides.
A program may use at most 64 MiB of HBM per device.

v0:
```python
import jax
import jax.numpy as jnp
import numpy as np
from jax import lax
from jax.sharding import Mesh
from jax.sharding import PartitionSpec as P

GLL = 4
SUBSTEPS = 2
BLK = ("blk_0", "blk_1", "blk_2")
FACE_BLK = ("face", "blk_0", "blk_1", "blk_2")


deriv_table = [
    [-3.0, 4.045084971874737, -1.545084971874737, 0.5],
    [-0.8090169943749475, 0.0, 1.118033988749895, -0.30901699437494745],
    [0.30901699437494745, -1.118033988749895, 0.0, 0.8090169943749475],
    [-0.5, 1.545084971874737, -4.045084971874737, 3.0],
]
time_step = 0.05
relax_rate = 0.3
flux_gain = 0.2


def with_halo(block, sides, width):
    for axis, dim in sides:
        count = lax.axis_size(axis)
        forward = [(i, i + 1) for i in range(count - 1)]
        forward.append((count - 1, 0))
        backward = [(target, source) for source, target in forward]
        low = lax.ppermute(
            lax.slice_in_dim(block, block.shape[dim] - width, None, axis=dim), axis, forward
        )
        high = lax.ppermute(lax.slice_in_dim(block, 0, width, axis=dim), axis, backward)
        block = jnp.concatenate([low, block, high], axis=dim)
    return block


def split_up(value, dim, peers):
    before, after = (value.shape[:dim], value.shape[dim + 1 :])
    return jnp.moveaxis(value.reshape(*before, peers, -1, *after), dim, 0)


def joined_along(parts, dim):
    shape = list(parts.shape[1:])
    shape[dim] *= parts.shape[0]
    return jnp.moveaxis(parts, 0, dim).reshape(shape)


def moved_by_axis(parts, axes, sequence):
    inside = parts.shape[1:]
    result = parts.reshape(*(lax.axis_size(a) for a in axes), *inside)
    for k in sequence:
        result = lax.all_to_all(result, axes[k], k, k, tiled=True)
    return result.reshape(-1, *inside)


def core_and_chips(value, groups, sequence, split_dim, concat_dim):
    peers = lax.axis_size(groups[0]) * lax.axis_size(groups[1])
    parts = split_up(value, split_dim, peers)
    return joined_along(moved_by_axis(parts, groups, sequence), concat_dim)


def along_first(field):
    planes, xsize, ysize = field.shape
    blocks = np.kron(np.eye(xsize // GLL), np.array(deriv_table))
    table = jnp.asarray(blocks, jnp.float32)
    return jnp.einsum("ik,aky->aiy", table, field, precision=lax.Precision.HIGHEST)


def along_second(field):
    planes, xsize, ysize = field.shape
    width = min(ysize, 128)
    blocks = np.kron(np.eye(width // GLL), np.array(deriv_table).T)
    table = jnp.asarray(blocks, jnp.float32)
    shaped = field.reshape(planes, xsize, ysize // width, width)
    result = jnp.einsum("axek,ki->axei", shaped, table, precision=lax.Precision.HIGHEST)
    return result.reshape(planes, xsize, ysize)


def sum_rows(widened):
    xsize = widened.shape[1] - 2
    x_pos = jnp.arange(xsize, dtype=jnp.int32) % GLL
    first_row = (x_pos == 0)[:, None]
    last_row = (x_pos == GLL - 1)[:, None]
    return (
        widened[:, 1:-1]
        + jnp.where(first_row, widened[:, :-2], 0.0)
        + jnp.where(last_row, widened[:, 2:], 0.0)
    )


def sum_cols(widened):
    ysize = widened.shape[2] - 2
    y_pos = jnp.arange(ysize, dtype=jnp.int32) % GLL
    first_col = y_pos == 0
    last_col = y_pos == GLL - 1
    return (
        widened[:, :, 1:-1]
        + jnp.where(first_col, widened[:, :, :-2], 0.0)
        + jnp.where(last_col, widened[:, :, 2:], 0.0)
    )


def edge_average(moved, mass_map):
    weighted = jnp.concatenate([mass_map[None] * moved, mass_map[None]], axis=0)
    widened = with_halo(weighted, (("face", 1),), 1)
    partial_sum = sum_rows(widened)
    widened_cols = with_halo(partial_sum, ((BLK, 2),), 1)
    summed = sum_cols(widened_cols)
    return summed[:-1] / summed[-1:]


def body(
    air_state,
    air_wind,
    jacobian,
    land_area,
    xgrid_rows,
    tracers,
    edge_coef,
    neighbours,
    vert_rate,
    ocean_area,
    send_list,
    xgrid_cols,
    xgrid_weights,
):
    field_count, levels, x_points, y_points = air_state.shape
    planes = field_count * levels
    cell_count = tracers.shape[2]
    send_ids = send_list[0]
    rim_width = send_ids.shape[0] // 2
    outgoing = tracers[:, :, send_ids]
    received = with_halo(outgoing, ((BLK, 2),), rim_width)
    extended = jnp.concatenate(
        [tracers, received[:, :, :rim_width], received[:, :, 3 * rim_width :]], axis=2
    )
    adjacent = extended[:, :, neighbours]
    lateral = jnp.sum(edge_coef[None, None] * (adjacent - tracers[:, :, None]), axis=2)
    upper_level = jnp.concatenate([tracers[:, :1], tracers[:, :-1]], axis=1)
    lower_level = jnp.concatenate([tracers[:, 1:], tracers[:, -1:]], axis=1)
    vertical = vert_rate * (upper_level - tracers + (lower_level - tracers))
    ocean_partial = tracers + lateral + vertical
    cell_ids = xgrid_cols[0]
    weights = xgrid_weights[0]
    point_ids = xgrid_rows[0].reshape(-1)
    surface_at = tracers[0, 0][cell_ids]
    payload = jnp.stack([weights * surface_at, weights])
    arrived = core_and_chips(payload, (("blk_0", "blk_1"), "blk_2"), (0, 1), 1, 1)
    sums = (
        jnp.zeros((2, x_points * y_points), jnp.float32)
        .at[:, point_ids]
        .add(arrived.reshape(2, -1))
    )
    heat_map = sums[0].reshape(x_points, y_points)
    frac_map = sums[1].reshape(x_points, y_points)
    t_surf = (heat_map + land_area * air_state[0, 0]) / (frac_map + land_area)
    x_pos = jnp.arange(x_points, dtype=jnp.int32) % GLL
    y_pos = jnp.arange(y_points, dtype=jnp.int32) % GLL
    x_weight = jnp.where((x_pos == 0) | (x_pos == GLL - 1), 1.0 / 6.0, 5.0 / 6.0).astype(
        jnp.float32
    )
    y_weight = jnp.where((y_pos == 0) | (y_pos == GLL - 1), 1.0 / 6.0, 5.0 / 6.0).astype(
        jnp.float32
    )
    mass_map = x_weight[:, None] * y_weight[None, :] * jacobian
    fields = air_state
    for substep in range(SUBSTEPS):
        flat_fields = fields.reshape(planes, x_points, y_points)
        slope_first = along_first(flat_fields).reshape(field_count, levels, x_points, y_points)
        slope_second = along_second(flat_fields).reshape(field_count, levels, x_points, y_points)
        tendency = -(air_wind[0] * slope_first + air_wind[1] * slope_second)
        moved = fields + time_step * tendency
        moved = moved.at[0, 0].add(relax_rate * (t_surf - fields[0, 0]))
        fields = edge_average(moved.reshape(planes, x_points, y_points), mass_map).reshape(
            field_count, levels, x_points, y_points
        )
    sea_flux = (fields[0, 0] - t_surf).reshape(-1)
    flux_slots = sea_flux[xgrid_rows[0]]
    incoming = core_and_chips(flux_slots, (("blk_0", "blk_1"), "blk_2"), (1, 0), 0, 0)
    inflow = (
        jnp.zeros((cell_count,), jnp.float32)
        .at[cell_ids.reshape(-1)]
        .add((weights * incoming).reshape(-1))
    )
    ocean_final = ocean_partial.at[0, 0].add(flux_gain * inflow / ocean_area)
    return (fields, ocean_final)


def solution(mesh):
    finer = Mesh(
        mesh.devices.reshape(mesh.shape["face"], 8, 4, 2), ("face", "blk_0", "blk_1", "blk_2")
    )
    in_specs = (
        P(None, None, "face", BLK),
        P(None, None, "face", BLK),
        P("face", BLK),
        P("face", BLK),
        P(FACE_BLK, None, None),
        P(None, None, FACE_BLK),
        P(None, FACE_BLK),
        P(None, FACE_BLK),
        P(FACE_BLK),
        P(FACE_BLK),
        P(FACE_BLK, None),
        P(FACE_BLK, None, None),
        P(FACE_BLK, None, None),
    )
    out_specs = (P(None, None, "face", BLK), P(None, None, FACE_BLK))
    return jax.shard_map(body, mesh=finer, in_specs=in_specs, out_specs=out_specs, check_vma=False)
```

profile of v0, /device:TPU:1, one launch (start us, length us, event | category | flops | bytes accessed | tf_op | source)
XLA Modules:
  0.0 412.9 jit_solution(15768268280761935464)
XLA Ops:
  2.3 45.5 %gather_fusion = f32[8192]{0:T(1024)S(1)} fusion(f32[2048]{0:T(1024)S(1)} %bitcast.141, s32[8192]{0:T(1024)S(1)} %fusion.37), kind=kCustom, calls=%fused_computation | custom fusion | bytes 98304 | tf_op jit(solution)/shard_map/gather | solution.py:148
  48.5 10.5 %all-to-all-start = ((f32[32,2,2,1,128]{4,1,2,3,0:T(2,128)}), f32[32,2,2,1,128]{4,1,2,3,0:T(2,128)S(1)}, u32[]{:S(2)}, u32[]{:S(2)}) async-start(f32[32,2,2,1,128]{4,1,2,3,0:T(2,128)} %copy.52), calls=%async_computation | async-start | bytes 131072 | tf_op jit(solution)/shard_map/all_to_all | solution.py:54
  59.0 1.0 copy.57
  61.8 10.8 %collective-permute-start.8 = (f32[2,16,128]{1,0,2:T(2,128)}, f32[2,16,128]{1,0,2:T(2,128)}, u32[]{:S(2)}, u32[]{:S(2)}) collective-permute-start(f32[2,16,128]{1,0,2:T(2,128)} %get-tuple-element.50), channel_id=1, source_target_pairs={{0,1},{1,2},{2,3},{3,4},{4,5},{5,6},{6,7},{7,8},{8,9},{9,10},{10,1... | collective-permute-start | bytes 49160 | tf_op jit(solution)/shard_map/ppermute | solution.py:31
  72.6 1.9 collective-permute-start.9
  76.0 1.4 fusion.39
  77.4 1.4 compare_select_fusion.1
  78.9 1.4 compare_select_fusion
  83.0 1.2 fusion.6
  84.3 7.2 %all_to_all.20 = f32[32,2,2,1,128]{4,0,2,3,1:T(8,128)S(1)} all-to-all(f32[32,2,2,1,128]{4,0,2,3,1:T(8,128)S(1)} %copy.53), channel_id=1, replica_groups=mesh['face'=16,'blk_0'=8,'blk_1'=4,'blk_2'=2] {'blk_2'}, dimensions={1} | all-to-all | bytes 131072 | tf_op jit(solution)/shard_map/all_to_all | solution.py:54
  91.6 2.6 copy.62
  94.2 44.5 %scatter_custom_fusion = f32[2,2048]{0,1:T(8,128)S(1)} fusion(s32[8192]{0:T(1024)} %bitcast.160, f32[8192,2]{1,0:T(8,128)} %bitcast.143, f32[]{:T(128)} %constant.146.clone.1), kind=kCustom, calls=%fused_computation.31 | custom fusion | flops 16384 | bytes 16896 | tf_op jit(solution)/shard_map/scatter-add | solution.py:154
  139.7 1.3 fusion.51
  142.1 1.9 collective-permute-start
  144.0 11.4 %collective-permute-start.1 = (f32[49,1,128]{2,1,0:T(1,128)S(1)}, f32[49,1,128]{2,1,0:T(1,128)S(1)}, u32[]{:S(2)}, u32[]{:S(2)}) collective-permute-start(f32[49,1,128]{2,1,0:T(1,128)S(1)} %get-tuple-element.49), channel_id=1, source_target_pairs={{64,0},{128,64},{192,128},{256,192},{320,256},{384,320},{448,384},... | collective-permute-start | bytes 75272 | tf_op jit(solution)/shard_map/ppermute | solution.py:34
  156.8 1.9 collective-permute-start.2
  158.7 3.1 collective-permute-start.3
  161.9 1.6 collective-permute-done.2
  163.5 4.7 %collective-permute-done.3 = f32[49,16,1]{2,1,0:T(8,128)S(1)} collective-permute-done((f32[49,16,1]{2,1,0:T(8,128)S(1)}, f32[49,16,1]{2,1,0:T(8,128)S(1)}, u32[]{:S(2)}, u32[]{:S(2)}) %collective-permute-start.3) | collective-permute-done | bytes 3168 | tf_op jit(solution)/shard_map/ppermute | solution.py:34
  169.8 1.9 collective-permute-start.4
  171.7 5.0 %collective-permute-start.5 = (f32[49,1,128]{2,1,0:T(1,128)S(1)}, f32[49,1,128]{2,1,0:T(1,128)S(1)}, u32[]{:S(2)}, u32[]{:S(2)}) collective-permute-start(f32[49,1,128]{2,1,0:T(1,128)S(1)} %get-tuple-element.45), channel_id=1, source_target_pairs={{64,0},{128,64},{192,128},{256,192},{320,256},{384,320},{448,384},... | collective-permute-start | bytes 75272 | tf_op jit(solution)/shard_map/ppermute | solution.py:34
  176.7 5.8 %pad_maximum_fusion = f32[2,16,2304]{1,0,2:T(2,128)} fusion(f32[2,16,128]{1,0,2:T(2,128)} %collective-permute-done.9, f32[2,16,128]{1,0,2:T(2,128)} %collective-permute-done.8, f32[2,16,2048]{1,0,2:T(2,128)S(1)} %copy.57), kind=kLoop, calls=%fused_computation.6 | loop fusion | flops 147456 | bytes 589824 | tf_op jit(solution)/shard_map/concatenate | solution.py:136
  182.5 85.5 %gather_fusion.2 = f32[12288,2,16]{2,1,0:T(2,128)} fusion(f32[2,16,2304]{1,0,2:T(2,128)} %pad_maximum_fusion, s32[12288]{0:T(1024)S(1)} %copy-done.10), kind=kCustom, calls=%fused_computation.2 | custom fusion | bytes 3194880 | tf_op jit(solution)/shard_map/gather | solution.py:139
  268.0 12.3 %copy.63 = f32[6,2048,2,16]{1,0,3,2:T(8,128)S(1)} copy(f32[6,2048,2,16]{3,2,1,0:T(2,128)} %bitcast.142) | data formatting | bytes 3145728 | tf_op jit(solution)/shard_map/gather | solution.py:139
  280.8 1.9 collective-permute-start.6
  282.8 6.8 %collective-permute-start.7 = (f32[49,16,1]{2,1,0:T(8,128)S(1)}, f32[49,16,1]{2,1,0:T(8,128)S(1)}, u32[]{:S(2)}, u32[]{:S(2)}) collective-permute-start(f32[49,16,1]{2,1,0:T(8,128)S(1)} %get-tuple-element.43), channel_id=1, source_target_pairs={{1,0},{2,1},{3,2},{4,3},{5,4},{6,5},{7,6},{8,7},{9,8},{10,9},{11,1... | collective-permute-start | bytes 9416 | tf_op jit(solution)/shard_map/ppermute | solution.py:34
  290.4 1.5 collective-permute-done.7
  292.5 45.5 %gather_fusion.3 = f32[8192]{0:T(1024)S(1)} fusion(f32[2048]{0:T(1024)S(1)} %fusion.45, s32[8192]{0:T(1024)S(1)} %copy-done.14), kind=kCustom, calls=%fused_computation.3 | custom fusion | bytes 98304 | tf_op jit(solution)/shard_map/gather | solution.py:180
  338.1 11.2 %all_to_all.21 = f32[32,2,1,128]{3,2,0,1:T(1,128)S(1)} all-to-all(f32[32,2,1,128]{3,2,0,1:T(1,128)S(1)} %copy.59), channel_id=1, replica_groups=mesh['face'=16,'blk_0'=8,'blk_1'=4,'blk_2'=2] {'blk_2'}, dimensions={1} | all-to-all | bytes 65536 | tf_op jit(solution)/shard_map/all_to_all | solution.py:54
  349.9 9.5 %all-to-all-start.3 = ((f32[32,2,1,128]{3,2,1,0:T(1,128)}), f32[32,2,1,128]{3,2,1,0:T(1,128)S(1)}, u32[]{:S(2)}, u32[]{:S(2)}) async-start(f32[32,2,1,128]{3,2,1,0:T(1,128)} %copy.60), calls=%async_computation.3 | async-start | bytes 65536 | tf_op jit(solution)/shard_map/all_to_all | solution.py:54
  359.7 8.5 %all-to-all-done.3 = f32[32,2,1,128]{3,2,1,0:T(1,128)S(1)} async-done(((f32[32,2,1,128]{3,2,1,0:T(1,128)}), f32[32,2,1,128]{3,2,1,0:T(1,128)S(1)}, u32[]{:S(2)}, u32[]{:S(2)}) %all-to-all-start.3) | async-done | bytes 32800 | tf_op jit(solution)/shard_map/all_to_all | solution.py:54
  368.2 43.7 %scatter_custom_fusion.1 = f32[2048]{0:T(1024)S(1)} fusion(s32[8192]{0:T(1024)} %bitcast.159, f32[8192]{0:T(1024)S(1)} %bitcast_multiply_fusion.2, f32[]{:T(128)} %constant.146.clone.1), kind=kCustom, calls=%fused_computation.113 | custom fusion | flops 8192 | bytes 8704 | tf_op jit(solution)/shard_map/scatter-add | solution.py:185
  (123 shorter events, 16.5 us)
Async XLA Ops:
  2.2 45.6 %copy-start.7 = (f32[1,64,128]{2,1,0:T(8,128)S(1)}, f32[1,64,128]{2,1,0:T(8,128)}, u32[]{:S(2)}) copy-start(f32[1,64,128]{2,1,0:T(8,128)} %param.35) | copy-start | bytes 98308
  2.3 56.7 %copy-start = (f32[2,16,2048]{2,1,0:T(8,128)S(1)}, f32[2,16,2048]{2,1,0:T(8,128)}, u32[]{:S(2)}) copy-start(f32[2,16,2048]{2,1,0:T(8,128)} %param.28) | copy-start | bytes 786436
  47.8 28.2 %copy-start.13 = (f32[2,16,16,128]{3,2,1,0:T(8,128)S(1)}, f32[2,16,16,128]{3,2,1,0:T(8,128)}, u32[]{:S(2)}) copy-start(f32[2,16,16,128]{3,2,1,0:T(8,128)} %param.24) | copy-start | bytes 786436
  48.5 35.8 %all-to-all-start = ((f32[32,2,2,1,128]{4,1,2,3,0:T(2,128)}), f32[32,2,2,1,128]{4,1,2,3,0:T(2,128)S(1)}, u32[]{:S(2)}, u32[]{:S(2)}) async-start(f32[32,2,2,1,128]{4,1,2,3,0:T(2,128)} %copy.52), calls=%async_computation | async-start | bytes 131072 | tf_op jit(solution)/shard_map/all_to_all | solution.py:54
  59.0 22.7 %copy-start.1 = (f32[3,16,16,128]{3,2,1,0:T(8,128)S(1)}, f32[3,16,16,128]{3,2,1,0:T(8,128)}, u32[]{:S(2)}) copy-start(f32[3,16,16,128]{3,2,1,0:T(8,128)} %param.23) | copy-start | bytes 1179652
  59.0 22.7 %copy-start.18 = (f32[16,16,1]{1,0,2:T(8,128)S(1)}, f32[16,16,1]{1,0,2:T(8,128)}, u32[]{:S(2)}) copy-start(f32[16,16,1]{1,0,2:T(8,128)} %constant.157) | copy-start | bytes 3076
  60.1 22.9 %copy-start.11 = (f32[128,128,1,1]{1,0,3,2:T(8,128)S(1)}, f32[128,128,1,1]{1,0,3,2:T(8,128)}, u32[]{:S(2)}) copy-start(f32[128,128,1,1]{1,0,3,2:T(8,128)} %constant.158) | copy-start | bytes 196612
  61.8 22.4 %copy-start.20 = (f32[16,128]{1,0:T(8,128)S(1)}, f32[16,128]{1,0:T(8,128)}, u32[]{:S(2)}) copy-start(f32[16,128]{1,0:T(8,128)} %param.25) | copy-start | bytes 24580
  61.8 114.9 %collective-permute-start.8 = (f32[2,16,128]{1,0,2:T(2,128)}, f32[2,16,128]{1,0,2:T(2,128)}, u32[]{:S(2)}, u32[]{:S(2)}) collective-permute-start(f32[2,16,128]{1,0,2:T(2,128)} %get-tuple-element.50), channel_id=1, source_target_pairs={{0,1},{1,2},{2,3},{3,4},{4,5},{5,6},{6,7},{7,8},{8,9},{9,10},{10,1... | collective-permute-start | bytes 49160 | tf_op jit(solution)/shard_map/ppermute | solution.py:31
  72.6 104.1 %collective-permute-start.9 = (f32[2,16,128]{1,0,2:T(2,128)}, f32[2,16,128]{1,0,2:T(2,128)}, u32[]{:S(2)}, u32[]{:S(2)}) collective-permute-start(f32[2,16,128]{1,0,2:T(2,128)} %get-tuple-element.51), channel_id=1, source_target_pairs={{1,0},{2,1},{3,2},{4,3},{5,4},{6,5},{7,6},{8,7},{9,8},{10,9},{11,1... | collective-permute-start | bytes 49160 | tf_op jit(solution)/shard_map/ppermute | solution.py:34
  76.0 18.2 %copy-start.2 = (f32[16,16,128]{2,1,0:T(8,128)}, f32[16,16,128]{2,1,0:T(8,128)S(1)}, u32[]{:S(2)}) copy-start(f32[16,16,128]{2,1,0:T(8,128)S(1)} %get-tuple-element.57) | copy-start | bytes 393220
  142.1 13.4 %collective-permute-start = (f32[49,1,128]{2,1,0:T(1,128)S(1)}, f32[49,1,128]{2,1,0:T(1,128)S(1)}, u32[]{:S(2)}, u32[]{:S(2)}) collective-permute-start(f32[49,1,128]{2,1,0:T(1,128)S(1)} %get-tuple-element.48), channel_id=1, source_target_pairs={{0,64},{64,128},{128,192},{192,256},{256,320},{320,384},{384,448},... | collective-permute-start | bytes 75272 | tf_op jit(solution)/shard_map/ppermute | solution.py:31
  144.0 12.4 %collective-permute-start.1 = (f32[49,1,128]{2,1,0:T(1,128)S(1)}, f32[49,1,128]{2,1,0:T(1,128)S(1)}, u32[]{:S(2)}, u32[]{:S(2)}) collective-permute-start(f32[49,1,128]{2,1,0:T(1,128)S(1)} %get-tuple-element.49), channel_id=1, source_target_pairs={{64,0},{128,64},{192,128},{256,192},{320,256},{384,320},{448,384},... | collective-permute-start | bytes 75272 | tf_op jit(solution)/shard_map/ppermute | solution.py:34
  155.5 13.2 %copy-start.27 = (pred[16]{0:T(512)(128)(4,1)}, pred[16]{0:T(512)(128)(4,1)S(1)}, u32[]{:S(2)}) copy-start(pred[16]{0:T(512)(128)(4,1)S(1)} %get-tuple-element.60) | copy-start | bytes 52
  155.5 13.2 %copy-start.29 = (pred[16]{0:T(512)(128)(4,1)}, pred[16]{0:T(512)(128)(4,1)S(1)}, u32[]{:S(2)}) copy-start(pred[16]{0:T(512)(128)(4,1)S(1)} %get-tuple-element.61) | copy-start | bytes 52
  156.6 12.6 %copy-start.3 = (f32[16,16,128]{2,1,0:T(8,128)S(1)}, f32[16,16,128]{2,1,0:T(8,128)}, u32[]{:S(2)}) copy-start(f32[16,16,128]{2,1,0:T(8,128)} %copy-done.2) | copy-start | bytes 393220
  156.6 12.6 %copy-start.12 = (f32[128,128,1,1]{1,0,3,2:T(8,128)S(1)}, f32[128,128,1,1]{1,0,3,2:T(8,128)}, u32[]{:S(2)}) copy-start(f32[128,128,1,1]{1,0,3,2:T(8,128)} %constant.158) | copy-start | bytes 196612
  156.8 6.7 %collective-permute-start.2 = (f32[49,16,1]{2,1,0:T(8,128)S(1)}, f32[49,16,1]{2,1,0:T(8,128)S(1)}, u32[]{:S(2)}, u32[]{:S(2)}) collective-permute-start(f32[49,16,1]{2,1,0:T(8,128)S(1)} %get-tuple-element.46), channel_id=1, source_target_pairs={{0,1},{1,2},{2,3},{3,4},{4,5},{5,6},{6,7},{7,8},{8,9},{9,10},{10,1... | collective-permute-start | bytes 9416 | tf_op jit(solution)/shard_map/ppermute | solution.py:31
  158.7 9.5 %collective-permute-start.3 = (f32[49,16,1]{2,1,0:T(8,128)S(1)}, f32[49,16,1]{2,1,0:T(8,128)S(1)}, u32[]{:S(2)}, u32[]{:S(2)}) collective-permute-start(f32[49,16,1]{2,1,0:T(8,128)S(1)} %get-tuple-element.47), channel_id=1, source_target_pairs={{1,0},{2,1},{3,2},{4,3},{5,4},{6,5},{7,6},{8,7},{9,8},{10,9},{11,1... | collective-permute-start | bytes 9416 | tf_op jit(solution)/shard_map/ppermute | solution.py:34
  169.8 110.6 %collective-permute-start.4 = (f32[49,1,128]{2,1,0:T(1,128)S(1)}, f32[49,1,128]{2,1,0:T(1,128)S(1)}, u32[]{:S(2)}, u32[]{:S(2)}) collective-permute-start(f32[49,1,128]{2,1,0:T(1,128)S(1)} %get-tuple-element.44), channel_id=1, source_target_pairs={{0,64},{64,128},{128,192},{192,256},{256,320},{320,384},{384,448},... | collective-permute-start | bytes 75272 | tf_op jit(solution)/shard_map/ppermute | solution.py:31
  171.7 108.7 %collective-permute-start.5 = (f32[49,1,128]{2,1,0:T(1,128)S(1)}, f32[49,1,128]{2,1,0:T(1,128)S(1)}, u32[]{:S(2)}, u32[]{:S(2)}) collective-permute-start(f32[49,1,128]{2,1,0:T(1,128)S(1)} %get-tuple-element.45), channel_id=1, source_target_pairs={{64,0},{128,64},{192,128},{256,192},{320,256},{384,320},{448,384},... | collective-permute-start | bytes 75272 | tf_op jit(solution)/shard_map/ppermute | solution.py:34
  280.8 9.6 %collective-permute-start.6 = (f32[49,16,1]{2,1,0:T(8,128)S(1)}, f32[49,16,1]{2,1,0:T(8,128)S(1)}, u32[]{:S(2)}, u32[]{:S(2)}) collective-permute-start(f32[49,16,1]{2,1,0:T(8,128)S(1)} %get-tuple-element.42), channel_id=1, source_target_pairs={{0,1},{1,2},{2,3},{3,4},{4,5},{5,6},{6,7},{7,8},{8,9},{9,10},{10,1... | collective-permute-start | bytes 9416 | tf_op jit(solution)/shard_map/ppermute | solution.py:31
  282.8 9.2 %collective-permute-start.7 = (f32[49,16,1]{2,1,0:T(8,128)S(1)}, f32[49,16,1]{2,1,0:T(8,128)S(1)}, u32[]{:S(2)}, u32[]{:S(2)}) collective-permute-start(f32[49,16,1]{2,1,0:T(8,128)S(1)} %get-tuple-element.43), channel_id=1, source_target_pairs={{1,0},{2,1},{3,2},{4,3},{5,4},{6,5},{7,6},{8,7},{9,8},{10,9},{11,1... | collective-permute-start | bytes 9416 | tf_op jit(solution)/shard_map/ppermute | solution.py:34
  292.4 45.7 %copy-start.6 = (f32[48,16,128]{2,1,0:T(8,128)}, f32[48,16,128]{2,1,0:T(8,128)S(1)}, u32[]{:S(2)}) copy-start(f32[48,16,128]{2,1,0:T(8,128)S(1)} %slice_divide_fusion) | copy-start | bytes 1179652
  292.4 67.1 %copy-start.4 = (f32[2,15,2048]{2,1,0:T(8,128)S(1)}, f32[2,15,2048]{2,1,0:T(8,128)}, u32[]{:S(2)}) copy-start(f32[2,15,2048]{2,1,0:T(8,128)} %get-tuple-element.52) | copy-start | bytes 737284
  292.4 67.1 %copy-start.5 = (f32[2,15,2048]{2,1,0:T(8,128)S(1)}, f32[2,15,2048]{2,1,0:T(8,128)}, u32[]{:S(2)}) copy-start(f32[2,15,2048]{2,1,0:T(8,128)} %get-tuple-element.53) | copy-start | bytes 737284
  292.5 67.1 %copy-start.15 = (f32[2,1,2048]{2,1,0:T(1,128)S(1)}, f32[2,1,2048]{2,1,0:T(1,128)}, u32[]{:S(2)}) copy-start(f32[2,1,2048]{2,1,0:T(1,128)} %get-tuple-element.54) | copy-start | bytes 49156
  292.5 67.1 %copy-start.16 = (f32[2,1,2048]{2,1,0:T(1,128)S(1)}, f32[2,1,2048]{2,1,0:T(1,128)}, u32[]{:S(2)}) copy-start(f32[2,1,2048]{2,1,0:T(1,128)} %get-tuple-element.55) | copy-start | bytes 49156
  292.5 67.1 %copy-start.21 = (f32[2048]{0:T(1024)S(1)}, f32[2048]{0:T(1024)}, u32[]{:S(2)}) copy-start(f32[2048]{0:T(1024)} %param.31) | copy-start | bytes 24580
  292.5 75.7 %copy-start.8 = (f32[1,64,128]{2,1,0:T(8,128)S(1)}, f32[1,64,128]{2,1,0:T(8,128)}, u32[]{:S(2)}) copy-start(f32[1,64,128]{2,1,0:T(8,128)} %param.35) | copy-start | bytes 98308
  292.5 119.4 %copy-start.22 = (f32[2048]{0:T(1024)S(1)}, f32[2048]{0:T(1024)}, u32[]{:S(2)}) copy-start(f32[2048]{0:T(1024)} %param.32) | copy-start | bytes 24580
  349.9 18.2 %all-to-all-start.3 = ((f32[32,2,1,128]{3,2,1,0:T(1,128)}), f32[32,2,1,128]{3,2,1,0:T(1,128)S(1)}, u32[]{:S(2)}, u32[]{:S(2)}) async-start(f32[32,2,1,128]{3,2,1,0:T(1,128)} %copy.60), calls=%async_computation.3 | async-start | bytes 65536 | tf_op jit(solution)/shard_map/all_to_all | solution.py:54
  (12 other events, 115.0 us)
where the time goes:
time: 414 us; the launch traced here: 413 us
  local copies, waits for them, and re-layouts  200 us (48%)
  other arithmetic  106 us (26%)
  starting transfers between devices  66.7 us (16%)
  blocking collectives  18.4 us (4%)
  waiting for transfers between devices  17.3 us (4%)
    gather x2, local copies, waits for them, and re-layouts, body(): adjacent = extended[:, :, neighbours]  97.8 us
    gather x1, local copies, waits for them, and re-layouts, body(): surface_at = tracers[0, 0][cell_ids]  45.5 us
    gather x1, local copies, waits for them, and re-layouts, body(): flux_slots = sea_flux[xgrid_rows[0]]  45.5 us
    scatter-add x1, other arithmetic, body(): sums = jnp.zeros((2, x_points * y_points), jnp.float32).at[:, point_ids]....  44.5 us
    scatter-add x1, other arithmetic, body(): inflow = jnp.zeros((cell_count,), jnp.float32).at[cell_ids.reshape(-1)].a...  43.7 us
    ppermute x5, starting transfers between devices, with_halo(): lax.ppermute(lax.slice_in_dim(block, 0, width, axis=dim), axis, backward)  28.2 us
    all_to_all x2, starting transfers between devices, moved_by_axis(): result = lax.all_to_all(result, axes[k], k, k, tiled=True)  20 us
    ppermute x5, starting transfers between devices, with_halo(): lax.ppermute(lax.slice_in_dim(block, block.shape[dim] - width, None, axis...  18.5 us
  transfers between devices with their start and end apart: 12, of which 5 were waited for; matrix products, arithmetic and copies ran while one was open for 41% of the time, Pallas kernels for 0%

commit v1 on v0

--- a/solution.py
+++ b/solution.py
@@ -2,6 +2,8 @@
 import jax.numpy as jnp
 import numpy as np
 from jax import lax
+from jax.experimental import pallas as pl
+from jax.experimental.pallas import tpu as pltpu
 from jax.sharding import Mesh
 from jax.sharding import PartitionSpec as P
 
@@ -109,6 +111,100 @@
     widened_cols = with_halo(partial_sum, ((BLK, 2),), 1)
     summed = sum_cols(widened_cols)
     return summed[:-1] / summed[-1:]
+
+
+def lane_gather(rows, idx):
+    hi = lax.shift_right_logical(idx, 7)
+    lo = lax.bitwise_and(idx, 127)
+    found = jnp.zeros(idx.shape, jnp.float32)
+    for h, row in enumerate(rows):
+        picked = jnp.take_along_axis(jnp.broadcast_to(row, idx.shape), lo, axis=1)
+        found = jnp.where(hi == h, picked, found)
+    return found
+
+
+def gather_kernel(table_ref, idx_ref, out_ref):
+    rows = [table_ref[h : h + 1, :] for h in range(table_ref.shape[0])]
+    for i in range(idx_ref.shape[0] // 8):
+        out_ref[8 * i : 8 * i + 8, :] = lane_gather(rows, idx_ref[8 * i : 8 * i + 8, :])
+
+
+def gather_points(table, idx):
+    return pl.pallas_call(
+        gather_kernel, out_shape=jax.ShapeDtypeStruct(idx.shape, jnp.float32), name="gather_points"
+    )(table, idx)
+
+
+def lateral_kernel(ext_ref, near_ref, coef_ref, out_ref):
+    planes, width = ext_ref.shape
+    groups = planes // 8
+
+    def block(j, carry):
+        here = pl.ds(pl.multiple_of(j * 128, 128), 128)
+        own = [ext_ref[8 * g : 8 * g + 8, here] for g in range(groups)]
+        lateral = [jnp.zeros((8, 128), jnp.float32) for g in range(groups)]
+        for e in range(near_ref.shape[0]):
+            idx = jnp.broadcast_to(near_ref[e : e + 1, here], (8, 128))
+            coef = jnp.broadcast_to(coef_ref[e : e + 1, here], (8, 128))
+            hi = lax.shift_right_logical(idx, 7)
+            lo = lax.bitwise_and(idx, 127)
+            found = [jnp.zeros((8, 128), jnp.float32) for g in range(groups)]
+            for h in range(width // 128):
+                mine = hi == h
+                for g in range(groups):
+                    tile = ext_ref[8 * g : 8 * g + 8, 128 * h : 128 * h + 128]
+                    found[g] = jnp.where(mine, jnp.take_along_axis(tile, lo, axis=1), found[g])
+            for g in range(groups):
+                lateral[g] = lateral[g] + coef * (found[g] - own[g])
+        for g in range(groups):
+            out_ref[8 * g : 8 * g + 8, here] = lateral[g]
+        return carry
+
+    lax.fori_loop(0, out_ref.shape[1] // 128, block, 0)
+
+
+def scatter_kernel(idx_ref, *refs):
+    value_refs, out_ref = refs[:-1], refs[-1]
+    rows = out_ref.shape[1]
+    lane_iota = lax.broadcasted_iota(jnp.int32, (128, 128), 0)
+    row_iota = lax.broadcasted_iota(jnp.int32, (rows, 128), 0)
+
+    def slots(r, total):
+        idx = idx_ref[pl.ds(r, 1), :]
+        lo = jnp.broadcast_to(lax.bitwise_and(idx, 127), (128, 128))
+        hot = jnp.where(lane_iota == lo, 1.0, 0.0).astype(jnp.bfloat16)
+        mine = jnp.broadcast_to(lax.shift_right_logical(idx, 7), (rows, 128)) == row_iota
+        parts = []
+        for ref in value_refs:
+            rest = jnp.where(mine, jnp.broadcast_to(ref[pl.ds(r, 1), :], (rows, 128)), 0.0)
+            for _ in range(3):
+                part = rest.astype(jnp.bfloat16)
+                parts.append(part)
+                rest = rest - part.astype(jnp.float32)
+        left = jnp.concatenate(parts, axis=0)
+        return total + lax.dot_general(
+            left, hot, (((1,), (1,)), ((), ())), preferred_element_type=jnp.float32
+        )
+
+    count = len(value_refs)
+    total = lax.fori_loop(
+        0, idx_ref.shape[0], slots, jnp.zeros((3 * count * rows, 128), jnp.float32)
+    )
+    for q in range(count):
+        first = 3 * q * rows
+        out_ref[q] = (
+            total[first : first + rows]
+            + total[first + rows : first + 2 * rows]
+            + total[first + 2 * rows : first + 3 * rows]
+        )
+
+
+def scatter_points(idx, values, rows):
+    return pl.pallas_call(
+        scatter_kernel,
+        out_shape=jax.ShapeDtypeStruct((len(values), rows, 128), jnp.float32),
+        name="scatter_points",
+    )(idx, *values)
 
 
 def body(
@@ -136,23 +232,21 @@
     extended = jnp.concatenate(
         [tracers, received[:, :, :rim_width], received[:, :, 3 * rim_width :]], axis=2
     )
-    adjacent = extended[:, :, neighbours]
-    lateral = jnp.sum(edge_coef[None, None] * (adjacent - tracers[:, :, None]), axis=2)
+    lateral = pl.pallas_call(
+        lateral_kernel,
+        out_shape=jax.ShapeDtypeStruct((tracers.shape[0] * tracers.shape[1], cell_count), jnp.float32),
+        name="lateral",
+    )(extended.reshape(-1, extended.shape[2]), neighbours, edge_coef).reshape(tracers.shape)
     upper_level = jnp.concatenate([tracers[:, :1], tracers[:, :-1]], axis=1)
     lower_level = jnp.concatenate([tracers[:, 1:], tracers[:, -1:]], axis=1)
     vertical = vert_rate * (upper_level - tracers + (lower_level - tracers))
     ocean_partial = tracers + lateral + vertical
     cell_ids = xgrid_cols[0]
     weights = xgrid_weights[0]
-    point_ids = xgrid_rows[0].reshape(-1)
-    surface_at = tracers[0, 0][cell_ids]
+    surface_at = gather_points(tracers[0, 0].reshape(-1, 128), cell_ids)
     payload = jnp.stack([weights * surface_at, weights])
     arrived = core_and_chips(payload, (("blk_0", "blk_1"), "blk_2"), (0, 1), 1, 1)
-    sums = (
-        jnp.zeros((2, x_points * y_points), jnp.float32)
-        .at[:, point_ids]
-        .add(arrived.reshape(2, -1))
-    )
+    sums = scatter_points(xgrid_rows[0], (arrived[0], arrived[1]), x_points)
     heat_map = sums[0].reshape(x_points, y_points)
     frac_map = sums[1].reshape(x_points, y_points)
     t_surf = (heat_map + land_area * air_state[0, 0]) / (frac_map + land_area)
@@ -176,14 +270,10 @@
         fields = edge_average(moved.reshape(planes, x_points, y_points), mass_map).reshape(
             field_count, levels, x_points, y_points
         )
-    sea_flux = (fields[0, 0] - t_surf).reshape(-1)
-    flux_slots = sea_flux[xgrid_rows[0]]
+    sea_flux = fields[0, 0] - t_surf
+    flux_slots = gather_points(sea_flux, xgrid_rows[0])
     incoming = core_and_chips(flux_slots, (("blk_0", "blk_1"), "blk_2"), (1, 0), 0, 0)
-    inflow = (
-        jnp.zeros((cell_count,), jnp.float32)
-        .at[cell_ids.reshape(-1)]
-        .add((weights * incoming).reshape(-1))
-    )
+    inflow = scatter_points(cell_ids, (weights * incoming,), cell_count // 128).reshape(-1)
     ocean_final = ocean_partial.at[0, 0].add(flux_gain * inflow / ocean_area)
     return (fields, ocean_final)
 

time: 414 us -> 154 us (0.37)
  local copies, waits for them, and re-layouts: 200 us -> 9.25 us
  other arithmetic: 106 us -> 6.62 us
  Pallas kernels: 0 us -> 36.7 us
    gather x4 -> x0, local copies, waits for them, and re-layouts: 189 us -> none  [the longest x2 97.8 us: body(): adjacent = extended[:, :, neighbours]]
    scatter-add x2 -> x0, other arithmetic: 88.3 us -> none  [the longest x1 44.5 us: body(): sums = jnp.zeros((2, x_points * y_points), jnp.float32).at[:, point_ids]....]
    pallas_call x0 -> x5, Pallas kernels: none -> 36.7 us  [the longest x2 23 us: scatter_points(): pl.pallas_call(scatter_kernel, out_shape=jax.ShapeDtypeStruct((len(values...]
    concatenate x1, other arithmetic: 5.8 us -> 0.74 us  [body(): jnp.concatenate([tracers, received[:, :, :rim_width], received[:, :, 3 *...]
  transfers between devices with their start and end apart: 12 -> 12, of which waited for: 5 -> 5; matrix products, arithmetic and copies ran while one was open for 41% -> 6% of each run, Pallas kernels for 0% -> 14%
where the time goes in v1:
time: 154 us; the launch traced here: 152 us
  starting transfers between devices  64.5 us (42%)
  Pallas kernels  36.7 us (24%)
  waiting for transfers between devices  16.6 us (11%)
  blocking collectives  15.7 us (10%)
  local copies, waits for them, and re-layouts  9.25 us (6%)
  other arithmetic  6.62 us (4%)
  matrix products  1.88 us (1%)
    ppermute x5, starting transfers between devices, with_halo(): lax.ppermute(lax.slice_in_dim(block, 0, width, axis=dim), axis, backward)  28 us
    pallas_call x2, Pallas kernels, scatter_points(): pl.pallas_call(scatter_kernel, out_shape=jax.ShapeDtypeStruct((len(values...  23 us
    ppermute x5, starting transfers between devices, with_halo(): lax.ppermute(lax.slice_in_dim(block, block.shape[dim] - width, None, axis...  18.7 us
    all_to_all x2, starting transfers between devices, moved_by_axis(): result = lax.all_to_all(result, axes[k], k, k, tiled=True)  17.7 us
    all_to_all x2, blocking collectives, moved_by_axis(): result = lax.all_to_all(result, axes[k], k, k, tiled=True)  15.7 us
    pallas_call x1, Pallas kernels, body(): pl.pallas_call(lateral_kernel, out_shape=jax.ShapeDtypeStruct((tracers.sh...  10.5 us
    all_to_all x2, waiting for transfers between devices, moved_by_axis(): result = lax.all_to_all(result, axes[k], k, k, tiled=True)  8.56 us
    ppermute x5, waiting for transfers between devices, with_halo(): lax.ppermute(lax.slice_in_dim(block, 0, width, axis=dim), axis, backward)  6.35 us
  transfers between devices with their start and end apart: 12, of which 5 were waited for; matrix products, arithmetic and copies ran while one was open for 6% of the time, Pallas kernels for 14%

profile of v1, /device:TPU:1, one launch (start us, length us, event | category | flops | bytes accessed | tf_op | source)
XLA Modules:
  0.0 152.3 jit_solution(3943729003007325316)
XLA Ops:
  0.7 1.5 slice.204
  2.1 1.6 %gather_points.2 = f32[64,128]{1,0:T(8,128)} custom-call(f32[16,128]{1,0:T(8,128)} %bitcast.147, s32[64,128]{1,0:T(8,128)} %bitcast.143), custom_call_target="tpu_custom_call" | custom-call | tf_op jit(solution)/shard_map/gather_points/pallas_call | solution.py:133
  3.8 0.8 fusion.32
  4.5 0.8 pad_maximum_fusion.11
  6.0 10.6 %all-to-all-start = ((f32[32,2,2,1,128]{4,1,2,3,0:T(2,128)}), f32[32,2,2,1,128]{4,1,2,3,0:T(2,128)S(1)}, u32[]{:S(2)}, u32[]{:S(2)}) async-start(f32[32,2,2,1,128]{4,1,2,3,0:T(2,128)} %copy.22), calls=%async_computation | async-start | bytes 131072 | tf_op jit(solution)/shard_map/all_to_all | solution.py:56
  16.6 2.5 %copy.25 = f32[2,16,2048]{1,0,2:T(2,128)S(1)} copy(f32[2,16,2048]{2,1,0:T(8,128)} %param.28) | data formatting | bytes 524288 | tf_op args[5]
  19.2 1.0 gather_fusion
  20.2 10.7 %collective-permute-start.8 = (f32[2,16,128]{1,0,2:T(2,128)S(1)}, f32[2,16,128]{1,0,2:T(2,128)S(1)}, u32[]{:S(2)}, u32[]{:S(2)}) collective-permute-start(f32[2,16,128]{1,0,2:T(2,128)S(1)} %get-tuple-element.48), channel_id=1, source_target_pairs={{0,1},{1,2},{2,3},{3,4},{4,5},{5,6},{6,7},{7,8},{8,9},{9,10},{10,1... | collective-permute-start | bytes 49160 | tf_op jit(solution)/shard_map/ppermute | solution.py:33
  30.8 1.9 %collective-permute-start.9 = (f32[2,16,128]{1,0,2:T(2,128)S(1)}, f32[2,16,128]{1,0,2:T(2,128)S(1)}, u32[]{:S(2)}, u32[]{:S(2)}) collective-permute-start(f32[2,16,128]{1,0,2:T(2,128)S(1)} %get-tuple-element.49), channel_id=1, source_target_pairs={{1,0},{2,1},{3,2},{4,3},{5,4},{6,5},{7,6},{8,7},{9,8},{10,9},{11,1... | collective-permute-start | bytes 49160 | tf_op jit(solution)/shard_map/ppermute | solution.py:36
  34.0 7.2 %all_to_all.20 = f32[32,2,2,1,128]{4,0,2,3,1:T(8,128)S(1)} all-to-all(f32[32,2,2,1,128]{4,0,2,3,1:T(8,128)S(1)} %copy.23), channel_id=1, replica_groups=mesh['face'=16,'blk_0'=8,'blk_1'=4,'blk_2'=2] {'blk_2'}, dimensions={1} | all-to-all | bytes 131072 | tf_op jit(solution)/shard_map/all_to_all | solution.py:56
  41.9 11.5 %scatter_points.2 = f32[2,16,128]{2,1,0:T(8,128)} custom-call(s32[64,128]{1,0:T(8,128)} %bitcast.140, f32[64,128]{1,0:T(8,128)} %get-tuple-element.57.refs_0_, f32[64,128]{1,0:T(8,128)} %get-tuple-element.56.refs_1_), custom_call_target="tpu_custom_call" | custom-call | tf_op jit(solution)/shard_map/scatter_points/pallas_call | solution.py:203
  53.5 0.7 fusion.46
  54.3 1.9 %collective-permute-start = (f32[49,1,128]{2,1,0:T(1,128)S(1)}, f32[49,1,128]{2,1,0:T(1,128)S(1)}, u32[]{:S(2)}, u32[]{:S(2)}) collective-permute-start(f32[49,1,128]{2,1,0:T(1,128)S(1)} %get-tuple-element.46), channel_id=1, source_target_pairs={{0,64},{64,128},{128,192},{192,256},{256,320},{320,384},{384,448},... | collective-permute-start | bytes 75272 | tf_op jit(solution)/shard_map/ppermute | solution.py:33
  56.2 11.4 %collective-permute-start.1 = (f32[49,1,128]{2,1,0:T(1,128)S(1)}, f32[49,1,128]{2,1,0:T(1,128)S(1)}, u32[]{:S(2)}, u32[]{:S(2)}) collective-permute-start(f32[49,1,128]{2,1,0:T(1,128)S(1)} %get-tuple-element.47), channel_id=1, source_target_pairs={{64,0},{128,64},{192,128},{256,192},{320,256},{384,320},{448,384},... | collective-permute-start | bytes 75272 | tf_op jit(solution)/shard_map/ppermute | solution.py:36
  67.7 0.9 collective-permute-done.1
  68.9 1.9 %collective-permute-start.2 = (f32[49,16,1]{2,1,0:T(8,128)S(1)}, f32[49,16,1]{2,1,0:T(8,128)S(1)}, u32[]{:S(2)}, u32[]{:S(2)}) collective-permute-start(f32[49,16,1]{2,1,0:T(8,128)S(1)} %get-tuple-element.44), channel_id=1, source_target_pairs={{0,1},{1,2},{2,3},{3,4},{4,5},{5,6},{6,7},{7,8},{8,9},{9,10},{10,1... | collective-permute-start | bytes 9416 | tf_op jit(solution)/shard_map/ppermute | solution.py:33
  70.9 3.1 %collective-permute-start.3 = (f32[49,16,1]{2,1,0:T(8,128)S(1)}, f32[49,16,1]{2,1,0:T(8,128)S(1)}, u32[]{:S(2)}, u32[]{:S(2)}) collective-permute-start(f32[49,16,1]{2,1,0:T(8,128)S(1)} %get-tuple-element.45), channel_id=1, source_target_pairs={{1,0},{2,1},{3,2},{4,3},{5,4},{6,5},{7,6},{8,7},{9,8},{10,9},{11,1... | collective-permute-start | bytes 9416 | tf_op jit(solution)/shard_map/ppermute | solution.py:36
  74.0 1.7 %collective-permute-done.2 = f32[49,16,1]{2,1,0:T(8,128)S(1)} collective-permute-done((f32[49,16,1]{2,1,0:T(8,128)S(1)}, f32[49,16,1]{2,1,0:T(8,128)S(1)}, u32[]{:S(2)}, u32[]{:S(2)}) %collective-permute-start.2) | collective-permute-done | bytes 3168 | tf_op jit(solution)/shard_map/ppermute | solution.py:33
  75.7 4.7 %collective-permute-done.3 = f32[49,16,1]{2,1,0:T(8,128)S(1)} collective-permute-done((f32[49,16,1]{2,1,0:T(8,128)S(1)}, f32[49,16,1]{2,1,0:T(8,128)S(1)}, u32[]{:S(2)}, u32[]{:S(2)}) %collective-permute-start.3) | collective-permute-done | bytes 3168 | tf_op jit(solution)/shard_map/ppermute | solution.py:36
  81.9 1.9 %collective-permute-start.4 = (f32[49,1,128]{2,1,0:T(1,128)S(1)}, f32[49,1,128]{2,1,0:T(1,128)S(1)}, u32[]{:S(2)}, u32[]{:S(2)}) collective-permute-start(f32[49,1,128]{2,1,0:T(1,128)S(1)} %get-tuple-element.42), channel_id=1, source_target_pairs={{0,64},{64,128},{128,192},{192,256},{256,320},{320,384},{384,448},... | collective-permute-start | bytes 75272 | tf_op jit(solution)/shard_map/ppermute | solution.py:33
  83.8 4.9 %collective-permute-start.5 = (f32[49,1,128]{2,1,0:T(1,128)S(1)}, f32[49,1,128]{2,1,0:T(1,128)S(1)}, u32[]{:S(2)}, u32[]{:S(2)}) collective-permute-start(f32[49,1,128]{2,1,0:T(1,128)S(1)} %get-tuple-element.43), channel_id=1, source_target_pairs={{64,0},{128,64},{192,128},{256,192},{320,256},{384,320},{448,384},... | collective-permute-start | bytes 75272 | tf_op jit(solution)/shard_map/ppermute | solution.py:36
  88.8 0.7 collective-permute-done.5
  90.0 2.3 %collective-permute-start.6 = (f32[49,16,1]{2,1,0:T(8,128)S(1)}, f32[49,16,1]{2,1,0:T(8,128)S(1)}, u32[]{:S(2)}, u32[]{:S(2)}) collective-permute-start(f32[49,16,1]{2,1,0:T(8,128)S(1)} %get-tuple-element.40), channel_id=1, source_target_pairs={{0,1},{1,2},{2,3},{3,4},{4,5},{5,6},{6,7},{7,8},{8,9},{9,10},{10,1... | collective-permute-start | bytes 9416 | tf_op jit(solution)/shard_map/ppermute | solution.py:33
  92.3 6.7 %collective-permute-start.7 = (f32[49,16,1]{2,1,0:T(8,128)S(1)}, f32[49,16,1]{2,1,0:T(8,128)S(1)}, u32[]{:S(2)}, u32[]{:S(2)}) collective-permute-start(f32[49,16,1]{2,1,0:T(8,128)S(1)} %get-tuple-element.41), channel_id=1, source_target_pairs={{1,0},{2,1},{3,2},{4,3},{5,4},{6,5},{7,6},{8,7},{9,8},{10,9},{11,1... | collective-permute-start | bytes 9416 | tf_op jit(solution)/shard_map/ppermute | solution.py:36
  99.0 0.7 pad_maximum_fusion.10
  99.7 10.5 %lateral.1 = f32[32,2048]{1,0:T(8,128)} custom-call(f32[32,2304]{1,0:T(8,128)} %bitcast.133, s32[6,2048]{1,0:T(8,128)} %near_ref.1, f32[6,2048]{1,0:T(8,128)} %coef_ref.1), custom_call_target="tpu_custom_call" | custom-call | tf_op jit(solution)/shard_map/lateral/pallas_call | solution.py:235
  111.4 1.6 %gather_points.3 = f32[64,128]{1,0:T(8,128)} custom-call(f32[16,128]{1,0:T(8,128)} %fusion.37.table_ref, s32[64,128]{1,0:T(8,128)} %bitcast.141), custom_call_target="tpu_custom_call" | custom-call | tf_op jit(solution)/shard_map/gather_points/pallas_call | solution.py:133
  113.0 0.8 copy.28
  113.7 8.4 %all_to_all.21 = f32[32,2,1,128]{3,0,2,1:T(8,128)S(1)} all-to-all(f32[32,2,1,128]{3,0,2,1:T(8,128)S(1)} %copy.28), channel_id=1, replica_groups=mesh['face'=16,'blk_0'=8,'blk_1'=4,'blk_2'=2] {'blk_2'}, dimensions={1} | all-to-all | bytes 65536 | tf_op jit(solution)/shard_map/all_to_all | solution.py:56
  122.8 7.1 %all-to-all-start.3 = ((f32[32,2,1,128]{3,1,2,0:T(2,128)}), f32[32,2,1,128]{3,1,2,0:T(2,128)S(1)}, u32[]{:S(2)}, u32[]{:S(2)}) async-start(f32[32,2,1,128]{3,1,2,0:T(2,128)} %copy.29), calls=%async_computation.3 | async-start | bytes 65536 | tf_op jit(solution)/shard_map/all_to_all | solution.py:56
  130.1 8.6 %all-to-all-done.3 = f32[32,2,1,128]{3,1,2,0:T(2,128)S(1)} async-done(((f32[32,2,1,128]{3,1,2,0:T(2,128)}), f32[32,2,1,128]{3,1,2,0:T(2,128)S(1)}, u32[]{:S(2)}, u32[]{:S(2)}) %all-to-all-start.3) | async-done | bytes 32800 | tf_op jit(solution)/shard_map/all_to_all | solution.py:56
  139.2 11.4 %scatter_points.3 = f32[1,16,128]{2,1,0:T(8,128)} custom-call(s32[64,128]{1,0:T(8,128)} %bitcast.144, f32[64,128]{1,0:T(8,128)} %bitcast_multiply_fusion.2.refs_0_), custom_call_target="tpu_custom_call" | custom-call | tf_op jit(solution)/shard_map/scatter_points/pallas_call | solution.py:203
  (79 shorter events, 9.1 us)
Async XLA Ops:
  0.6 32.2 %copy-start = (f32[2,16,2048]{2,1,0:T(8,128)S(1)}, f32[2,16,2048]{2,1,0:T(8,128)}, u32[]{:S(2)}) copy-start(f32[2,16,2048]{2,1,0:T(8,128)} %param.28) | copy-start | bytes 786436
  0.6 18.5 %copy-start.13 = (s32[1,256]{1,0:T(1,128)S(1)}, s32[1,256]{1,0:T(1,128)}, u32[]{:S(2)}) copy-start(s32[1,256]{1,0:T(1,128)} %param.33) | copy-start | bytes 3076
  6.0 26.9 %copy-start.7 = (f32[2,16,16,128]{3,2,1,0:T(8,128)S(1)}, f32[2,16,16,128]{3,2,1,0:T(8,128)}, u32[]{:S(2)}) copy-start(f32[2,16,16,128]{3,2,1,0:T(8,128)} %param.24) | copy-start | bytes 786436
  6.0 28.1 %all-to-all-start = ((f32[32,2,2,1,128]{4,1,2,3,0:T(2,128)}), f32[32,2,2,1,128]{4,1,2,3,0:T(2,128)S(1)}, u32[]{:S(2)}, u32[]{:S(2)}) async-start(f32[32,2,2,1,128]{4,1,2,3,0:T(2,128)} %copy.22), calls=%async_computation | async-start | bytes 131072 | tf_op jit(solution)/shard_map/all_to_all | solution.py:56
  16.6 16.3 %copy-start.1 = (f32[3,16,16,128]{3,2,1,0:T(8,128)S(1)}, f32[3,16,16,128]{3,2,1,0:T(8,128)}, u32[]{:S(2)}) copy-start(f32[3,16,16,128]{3,2,1,0:T(8,128)} %param.23) | copy-start | bytes 1179652
  16.6 16.3 %copy-start.8 = (f32[16,16,1]{1,0,2:T(8,128)S(1)}, f32[16,16,1]{1,0,2:T(8,128)}, u32[]{:S(2)}) copy-start(f32[16,16,1]{1,0,2:T(8,128)} %constant.148) | copy-start | bytes 3076
  16.6 16.8 %copy-start.9 = (f32[16,128]{1,0:T(8,128)S(1)}, f32[16,128]{1,0:T(8,128)}, u32[]{:S(2)}) copy-start(f32[16,128]{1,0:T(8,128)} %param.25) | copy-start | bytes 24580
  16.6 16.8 %copy-start.6 = (f32[128,128,1,1]{1,0,3,2:T(8,128)S(1)}, f32[128,128,1,1]{1,0,3,2:T(8,128)}, u32[]{:S(2)}) copy-start(f32[128,128,1,1]{1,0,3,2:T(8,128)} %constant.149) | copy-start | bytes 196612
  20.2 68.5 %collective-permute-start.8 = (f32[2,16,128]{1,0,2:T(2,128)S(1)}, f32[2,16,128]{1,0,2:T(2,128)S(1)}, u32[]{:S(2)}, u32[]{:S(2)}) collective-permute-start(f32[2,16,128]{1,0,2:T(2,128)S(1)} %get-tuple-element.48), channel_id=1, source_target_pairs={{0,1},{1,2},{2,3},{3,4},{4,5},{5,6},{6,7},{7,8},{8,9},{9,10},{10,1... | collective-permute-start | bytes 49160 | tf_op jit(solution)/shard_map/ppermute | solution.py:33
  30.8 57.9 %collective-permute-start.9 = (f32[2,16,128]{1,0,2:T(2,128)S(1)}, f32[2,16,128]{1,0,2:T(2,128)S(1)}, u32[]{:S(2)}, u32[]{:S(2)}) collective-permute-start(f32[2,16,128]{1,0,2:T(2,128)S(1)} %get-tuple-element.49), channel_id=1, source_target_pairs={{1,0},{2,1},{3,2},{4,3},{5,4},{6,5},{7,6},{8,7},{9,8},{10,9},{11,1... | collective-permute-start | bytes 49160 | tf_op jit(solution)/shard_map/ppermute | solution.py:36
  32.8 20.7 %copy-start.11 = (f32[16,128]{1,0:T(8,128)S(1)}, f32[16,128]{1,0:T(8,128)}, u32[]{:S(2)}) copy-start(f32[16,128]{1,0:T(8,128)} %param.26) | copy-start | bytes 24580
  54.3 13.4 %collective-permute-start = (f32[49,1,128]{2,1,0:T(1,128)S(1)}, f32[49,1,128]{2,1,0:T(1,128)S(1)}, u32[]{:S(2)}, u32[]{:S(2)}) collective-permute-start(f32[49,1,128]{2,1,0:T(1,128)S(1)} %get-tuple-element.46), channel_id=1, source_target_pairs={{0,64},{64,128},{128,192},{192,256},{256,320},{320,384},{384,448},... | collective-permute-start | bytes 75272 | tf_op jit(solution)/shard_map/ppermute | solution.py:33
  56.2 12.4 %collective-permute-start.1 = (f32[49,1,128]{2,1,0:T(1,128)S(1)}, f32[49,1,128]{2,1,0:T(1,128)S(1)}, u32[]{:S(2)}, u32[]{:S(2)}) collective-permute-start(f32[49,1,128]{2,1,0:T(1,128)S(1)} %get-tuple-element.47), channel_id=1, source_target_pairs={{64,0},{128,64},{192,128},{256,192},{320,256},{384,320},{448,384},... | collective-permute-start | bytes 75272 | tf_op jit(solution)/shard_map/ppermute | solution.py:36
  68.9 6.7 %collective-permute-start.2 = (f32[49,16,1]{2,1,0:T(8,128)S(1)}, f32[49,16,1]{2,1,0:T(8,128)S(1)}, u32[]{:S(2)}, u32[]{:S(2)}) collective-permute-start(f32[49,16,1]{2,1,0:T(8,128)S(1)} %get-tuple-element.44), channel_id=1, source_target_pairs={{0,1},{1,2},{2,3},{3,4},{4,5},{5,6},{6,7},{7,8},{8,9},{9,10},{10,1... | collective-permute-start | bytes 9416 | tf_op jit(solution)/shard_map/ppermute | solution.py:33
  70.9 9.5 %collective-permute-start.3 = (f32[49,16,1]{2,1,0:T(8,128)S(1)}, f32[49,16,1]{2,1,0:T(8,128)S(1)}, u32[]{:S(2)}, u32[]{:S(2)}) collective-permute-start(f32[49,16,1]{2,1,0:T(8,128)S(1)} %get-tuple-element.45), channel_id=1, source_target_pairs={{1,0},{2,1},{3,2},{4,3},{5,4},{6,5},{7,6},{8,7},{9,8},{10,9},{11,1... | collective-permute-start | bytes 9416 | tf_op jit(solution)/shard_map/ppermute | solution.py:36
  81.9 7.0 %collective-permute-start.4 = (f32[49,1,128]{2,1,0:T(1,128)S(1)}, f32[49,1,128]{2,1,0:T(1,128)S(1)}, u32[]{:S(2)}, u32[]{:S(2)}) collective-permute-start(f32[49,1,128]{2,1,0:T(1,128)S(1)} %get-tuple-element.42), channel_id=1, source_target_pairs={{0,64},{64,128},{128,192},{192,256},{256,320},{320,384},{384,448},... | collective-permute-start | bytes 75272 | tf_op jit(solution)/shard_map/ppermute | solution.py:33
  83.8 5.8 %collective-permute-start.5 = (f32[49,1,128]{2,1,0:T(1,128)S(1)}, f32[49,1,128]{2,1,0:T(1,128)S(1)}, u32[]{:S(2)}, u32[]{:S(2)}) collective-permute-start(f32[49,1,128]{2,1,0:T(1,128)S(1)} %get-tuple-element.43), channel_id=1, source_target_pairs={{64,0},{128,64},{192,128},{256,192},{320,256},{384,320},{448,384},... | collective-permute-start | bytes 75272 | tf_op jit(solution)/shard_map/ppermute | solution.py:36
  89.9 40.0 %copy-start.10 = (f32[2048]{0:T(1024)S(1)}, f32[2048]{0:T(1024)}, u32[]{:S(2)}) copy-start(f32[2048]{0:T(1024)} %param.31) | copy-start | bytes 24580
  90.0 20.3 %collective-permute-start.6 = (f32[49,16,1]{2,1,0:T(8,128)S(1)}, f32[49,16,1]{2,1,0:T(8,128)S(1)}, u32[]{:S(2)}, u32[]{:S(2)}) collective-permute-start(f32[49,16,1]{2,1,0:T(8,128)S(1)} %get-tuple-element.40), channel_id=1, source_target_pairs={{0,1},{1,2},{2,3},{3,4},{4,5},{5,6},{6,7},{7,8},{8,9},{9,10},{10,1... | collective-permute-start | bytes 9416 | tf_op jit(solution)/shard_map/ppermute | solution.py:33
  92.3 18.0 %collective-permute-start.7 = (f32[49,16,1]{2,1,0:T(8,128)S(1)}, f32[49,16,1]{2,1,0:T(8,128)S(1)}, u32[]{:S(2)}, u32[]{:S(2)}) collective-permute-start(f32[49,16,1]{2,1,0:T(8,128)S(1)} %get-tuple-element.41), channel_id=1, source_target_pairs={{1,0},{2,1},{3,2},{4,3},{5,4},{6,5},{7,6},{8,7},{9,8},{10,9},{11,1... | collective-permute-start | bytes 9416 | tf_op jit(solution)/shard_map/ppermute | solution.py:36
  110.3 19.6 %copy-start.2 = (f32[32,2048]{1,0:T(8,128)S(1)}, f32[32,2048]{1,0:T(8,128)}, u32[]{:S(2)}) copy-start(f32[32,2048]{1,0:T(8,128)} %lateral.1) | copy-start | bytes 786436
  110.3 28.3 %copy-start.4 = (f32[1,64,128]{2,1,0:T(8,128)S(1)}, f32[1,64,128]{2,1,0:T(8,128)}, u32[]{:S(2)}) copy-start(f32[1,64,128]{2,1,0:T(8,128)} %param.35) | copy-start | bytes 98308
  110.3 40.4 %copy-start.12 = (f32[2048]{0:T(1024)S(1)}, f32[2048]{0:T(1024)}, u32[]{:S(2)}) copy-start(f32[2048]{0:T(1024)} %param.32) | copy-start | bytes 24580
  110.7 40.9 %copy-start.3 = (f32[48,16,128]{2,1,0:T(8,128)}, f32[48,16,128]{2,1,0:T(8,128)S(1)}, u32[]{:S(2)}) copy-start(f32[48,16,128]{2,1,0:T(8,128)S(1)} %slice_divide_fusion) | copy-start | bytes 1179652
  122.8 15.8 %all-to-all-start.3 = ((f32[32,2,1,128]{3,1,2,0:T(2,128)}), f32[32,2,1,128]{3,1,2,0:T(2,128)S(1)}, u32[]{:S(2)}, u32[]{:S(2)}) async-start(f32[32,2,1,128]{3,1,2,0:T(2,128)} %copy.29), calls=%async_computation.3 | async-start | bytes 65536 | tf_op jit(solution)/shard_map/all_to_all | solution.py:56
  151.6 0.7 copy-start.5

commit v2 on v0

v2 whole, which is shorter than its diff:
```python
import jax
import jax.numpy as jnp
from jax import lax
from jax.experimental import pallas as pl
from jax.experimental.pallas import tpu as pltpu
from jax.sharding import PartitionSpec as P

GLL = 4
DERIV = (
    (-3.0, 4.045084971874737, -1.545084971874737, 0.5),
    (-0.8090169943749475, 0.0, 1.118033988749895, -0.30901699437494745),
    (0.30901699437494745, -1.118033988749895, 0.0, 0.8090169943749475),
    (-0.5, 1.545084971874737, -4.045084971874737, 3.0),
)
TIME_STEP = 0.05
RELAX = 0.3
FLUX_GAIN = 0.2
DIRECTIONS = ((-1, 0), (1, 0), (0, -1), (0, 1), (-1, -1), (-1, 1), (1, -1), (1, 1))
REVERSE = (1, 0, 3, 2, 7, 6, 5, 4)
MARGIN_ROWS = {-1: (0, 8), 1: (8, 16), 0: (0, 16)}
MESH = pl.DeviceIdType.MESH
F32 = jnp.float32
BF16 = jnp.bfloat16
TILE = (8, 128)


def lane_gather(rows, hi, lo):
    found = jnp.zeros(TILE, F32)
    for h, row in enumerate(rows):
        found = jnp.where(hi == h, jnp.take_along_axis(row, lo, axis=1), found)
    return found


def tap_table(position, shift):
    table = jnp.zeros(TILE, F32)
    for i in range(GLL):
        if 0 <= i + shift < GLL:
            table = jnp.where(position == i, F32(DERIV[i][i + shift]), table)
    return table


def build_hot(idx_ref, hot_ref):
    rows = lax.broadcasted_iota(jnp.int32, (128, 128), 0)

    def step(r8, carry):
        base = pl.multiple_of(r8 * 8, 8)
        for i in range(8):
            lo = lax.bitwise_and(idx_ref[pl.ds(base + i, 1), :], 127)
            hot = jnp.where(rows == jnp.broadcast_to(lo, (128, 128)), 1.0, 0.0).astype(BF16)
            hot_ref[:, pl.ds(pl.multiple_of((base + i) * 128, 128), 128)] = hot
        return carry

    lax.fori_loop(0, idx_ref.shape[0] // 8, step, 0)


def build_left(idx_ref, values_at, left_ref):
    rows = lax.broadcasted_iota(jnp.int32, (16, 128), 0)

    def step(r8, carry):
        base = pl.multiple_of(r8 * 8, 8)
        hi = lax.shift_right_logical(idx_ref[pl.ds(base, 8), :], 7)
        parts = []
        for rest in values_at(base):
            for _ in range(3):
                part = rest.astype(BF16).astype(F32)
                parts.append(part)
                rest = rest - part
        for i in range(8):
            mine = jnp.broadcast_to(hi[i : i + 1], (16, 128)) == rows
            left = [
                jnp.where(mine, jnp.broadcast_to(p[i : i + 1], (16, 128)), 0.0).astype(BF16)
                for p in parts
            ]
            left_ref[0 : 16 * len(parts), pl.ds(pl.multiple_of((base + i) * 128, 128), 128)] = (
                jnp.concatenate(left, axis=0)
            )
        return carry

    lax.fori_loop(0, idx_ref.shape[0] // 8, step, 0)


def scatter_sums(left_ref, hot_ref, count):
    total = lax.dot_general(
        left_ref[0 : 48 * count, :],
        hot_ref[...],
        (((1,), (1,)), ((), ())),
        preferred_element_type=F32,
    )
    return [
        total[48 * q : 48 * q + 16] + total[48 * q + 16 : 48 * q + 32] + total[48 * q + 32 : 48 * q + 48]
        for q in range(count)
    ]


def interval_kernel(
    n_face,
    n_blk,
    air_ref,
    wind_ref,
    jac_ref,
    land_ref,
    rows_ref,
    tracer_ref,
    coef_ref,
    near_ref,
    vert_ref,
    area_ref,
    send_ref,
    cols_ref,
    weight_ref,
    air_out,
    ocean_out,
    heat_pay,
    heat_in,
    flux_pay,
    flux_in,
    rim_pay,
    rim_in,
    margin_pay,
    margin_in,
    surf_pay,
    surf_in,
    weighted_1,
    weighted_2,
    row_sum,
    column_pay_1,
    column_in_1,
    column_pay_2,
    column_in_2,
    field_1,
    mass_ref,
    inverse_ref,
    hot_rows,
    hot_cols,
    left_ref,
    base_ref,
    wide_ref,
    all_send,
    all_recv,
    near_send,
    near_recv,
):
    face, blk = lax.axis_index("face"), lax.axis_index("blk")

    def step_to(d):
        df, db = DIRECTIONS[d]
        return (lax.rem(face + df + n_face, n_face), lax.rem(blk + db + n_blk, n_blk))

    barrier = pltpu.get_barrier_semaphore()

    def greet(k, carry):
        peer = lax.rem(blk + k, n_blk)
        pl.semaphore_signal(barrier, inc=1, device_id=(face, peer), device_id_type=MESH)
        return carry

    lax.fori_loop(1, n_blk, greet, 0)
    for d in (0, 1, 4, 5, 6, 7):
        pl.semaphore_signal(barrier, inc=1, device_id=step_to(d), device_id_type=MESH)

    sub = lax.broadcasted_iota(jnp.int32, TILE, 0)
    lane = lax.broadcasted_iota(jnp.int32, TILE, 1)
    x_pos, y_pos = lax.bitwise_and(sub, 3), lax.bitwise_and(lane, 3)
    first_x, last_x = x_pos == 0, x_pos == 3
    first_y, last_y = y_pos == 0, y_pos == 3
    sixth, five_sixths = F32(1.0 / 6.0), F32(5.0 / 6.0)
    gll_weight = jnp.where(first_x | last_x, sixth, five_sixths) * jnp.where(
        first_y | last_y, sixth, five_sixths
    )
    shifts = (-3, -2, -1, 1, 2, 3)

    surface = [
        jnp.broadcast_to(tracer_ref[0:1, 128 * h : 128 * h + 128], TILE) for h in range(16)
    ]
    for i in range(n_blk // 8):
        idx = cols_ref[8 * i : 8 * i + 8, :]
        weight = weight_ref[8 * i : 8 * i + 8, :]
        at = lane_gather(surface, lax.shift_right_logical(idx, 7), lax.bitwise_and(idx, 127))
        heat_pay[8 * i : 8 * i + 8, 0, :] = weight * at
        heat_pay[8 * i : 8 * i + 8, 1, :] = weight

    for side in range(2):
        idx = jnp.broadcast_to(send_ref[side : side + 1, :], TILE)
        hi, lo = lax.shift_right_logical(idx, 7), lax.bitwise_and(idx, 127)
        for g in range(4):
            tiles = [tracer_ref[8 * g : 8 * g + 8, 128 * h : 128 * h + 128] for h in range(16)]
            rim_pay[side, 8 * g : 8 * g + 8, :] = lane_gather(tiles, hi, lo)

    margin_pay[0] = air_ref[0:16, :]
    margin_pay[1] = wind_ref[0:16, :]
    margin_pay[2] = wind_ref[256:272, :]
    margin_pay[3] = jac_ref[...]
    for half in range(2):
        mass_ref[8 * half : 8 * half + 8, :] = gll_weight * jac_ref[8 * half : 8 * half + 8, :]

    taps_y = [(s, tap_table(y_pos, s)) for s in shifts]
    centre_y = tap_table(y_pos, 0)

    def slope_y(v):
        total = centre_y * v
        for s, tap in taps_y:
            total = total + tap * pltpu.roll(v, (-s) % 128, 1)
        return total

    def advance(field_at, target):
        def group(g, carry):
            half = lax.rem(g, 2) * 128
            planes = pl.ds(pl.multiple_of(g * 8, 8), 8)
            for e in range(4):
                fields = [field_at(g, 4 * e + k) for k in range(4)]
                for i in range(4):
                    x = 4 * e + i
                    slope_x = None
                    for k in range(4):
                        if DERIV[i][k]:
                            term = F32(DERIV[i][k]) * fields[k]
                            slope_x = term if slope_x is None else slope_x + term
                    wind_x = wind_ref[pl.ds(half + x, 8, stride=16), :]
                    wind_y = wind_ref[pl.ds(half + 256 + x, 8, stride=16), :]
                    tendency = wind_x * slope_x + wind_y * slope_y(fields[i])
                    moved = fields[i] - F32(TIME_STEP) * tendency
                    mass = jnp.broadcast_to(mass_ref[x : x + 1, :], TILE)
                    target[x + 1, planes, :] = mass * moved
            return carry

        lax.fori_loop(0, 6, group, 0)

    advance(lambda g, x: air_ref[pl.ds(g * 128 + x, 8, stride=16), :], weighted_1)
    build_hot(rows_ref, hot_rows)

    pl.semaphore_wait(barrier, n_blk - 1 + 6)

    def exchange(pay, inbox, slot):
        def send(k, carry):
            peer = lax.rem(blk + k, n_blk)
            pltpu.make_async_remote_copy(
                src_ref=pay.at[peer],
                dst_ref=inbox.at[blk],
                send_sem=all_send.at[slot],
                recv_sem=all_recv.at[slot],
                device_id=(face, peer),
                device_id_type=MESH,
            ).start()
            return carry

        lax.fori_loop(1, n_blk, send, 0)

    def await_all(ref, sem):
        rest = ref.at[pl.ds(0, n_blk - 1)]
        pltpu.make_async_copy(rest, rest, sem).wait()

    started = []

    def send_near(src, dst, d, slot):
        copy = pltpu.make_async_remote_copy(
            src_ref=src,
            dst_ref=dst,
            send_sem=near_send.at[slot],
            recv_sem=near_recv.at[slot],
            device_id=step_to(d),
            device_id_type=MESH,
        )
        copy.start()
        started.append(copy)
        return copy

    exchange(heat_pay, heat_in, 0)
    margin_copies, surf_copies = [], []
    for d in range(8):
        low, high = MARGIN_ROWS[DIRECTIONS[d][0]]
        margin_copies.append(
            send_near(
                margin_pay.at[:, low:high, :],
                margin_in.at[REVERSE[d], :, 0 : high - low, :],
                d,
                d,
            )
        )
    row_copies = [
        send_near(weighted_1.at[1], weighted_1.at[17], 0, 16),
        send_near(weighted_1.at[16], weighted_1.at[0], 1, 17),
    ]
    rim_copies = [
        send_near(rim_pay.at[0], rim_in.at[1], 2, 24),
        send_near(rim_pay.at[1], rim_in.at[0], 3, 25),
    ]
    heat_in[blk] = heat_pay[blk]

    def ocean(first, last):
        def block(j, carry):
            here = pl.ds(pl.multiple_of(j * 128, 128), 128)
            own = [tracer_ref[8 * g : 8 * g + 8, here] for g in range(4)]
            lateral = [jnp.zeros(TILE, F32) for g in range(4)]
            for e in range(6):
                idx = jnp.broadcast_to(near_ref[e : e + 1, here], TILE)
                coef = jnp.broadcast_to(coef_ref[e : e + 1, here], TILE)
                hi, lo = lax.shift_right_logical(idx, 7), lax.bitwise_and(idx, 127)
                found = [jnp.zeros(TILE, F32) for g in range(4)]
                for h in range(18):
                    mine = hi == h
                    for g in range(4):
                        if h < 16:
                            tile = tracer_ref[8 * g : 8 * g + 8, 128 * h : 128 * h + 128]
                        else:
                            tile = rim_in[h - 16, 8 * g : 8 * g + 8, :]
                        found[g] = jnp.where(mine, jnp.take_along_axis(tile, lo, axis=1), found[g])
                for g in range(4):
                    lateral[g] = lateral[g] + coef * (found[g] - own[g])
            rate = jnp.broadcast_to(vert_ref[pl.ds(j, 1), :], TILE)
            for t in range(2):
                top, low = own[2 * t], own[2 * t + 1]
                down = [pltpu.roll(v, 1, 0) for v in (top, low)]
                up = [pltpu.roll(v, 7, 0) for v in (top, low)]
                above = [jnp.where(sub == 0, top, down[0]), jnp.where(sub == 0, down[0], down[1])]
                below = [jnp.where(sub == 7, up[1], up[0]), jnp.where(sub == 7, low, up[1])]
                for i, v in enumerate((top, low)):
                    g = 2 * t + i
                    vertical = rate * ((above[i] - v) + (below[i] - v))
                    ocean_out[8 * g : 8 * g + 8, here] = v + lateral[g] + vertical
            return carry

        lax.fori_loop(first, last, block, 0)

    def sum_rows(weighted, column_pay):
        def group(g, carry):
            planes = pl.ds(pl.multiple_of(g * 8, 8), 8)
            packed = [jnp.zeros(TILE, F32), jnp.zeros(TILE, F32)]
            for x in range(16):
                total = weighted[x + 1, planes, :]
                if x % 4 == 0:
                    total = total + weighted[x, planes, :]
                if x % 4 == 3:
                    total = total + weighted[x + 2, planes, :]
                row_sum[x, planes, :] = total
                packed[0] = jnp.where(lane == x, pltpu.roll(total, x, 1), packed[0])
                packed[1] = jnp.where(lane == x, pltpu.roll(total, x + 1, 1), packed[1])
            for side in range(2):
                column_pay[side, planes, :] = packed[side]
            return carry

        lax.fori_loop(0, 6, group, 0)

    def sum_columns(column_in, store):
        def group(g, carry):
            planes = pl.ds(pl.multiple_of(g * 8, 8), 8)
            left, right = column_in[0, planes, :], column_in[1, planes, :]
            for x in range(16):
                v = row_sum[x, planes, :]
                before = jnp.where(
                    lane == 0, pltpu.roll(left, (128 - x) % 128, 1), pltpu.roll(v, 1, 1)
                )
                after = jnp.where(
                    lane == 127, pltpu.roll(right, 127 - x, 1), pltpu.roll(v, 127, 1)
                )
                total = v + jnp.where(first_y, before, 0.0) + jnp.where(last_y, after, 0.0)
                store(g, x, total * jnp.broadcast_to(inverse_ref[x : x + 1, :], TILE))
            return carry

        lax.fori_loop(0, 6, group, 0)

    for copy in row_copies:
        copy.wait_recv()
    sum_rows(weighted_1, column_pay_1)
    column_copies = [
        send_near(column_pay_1.at[0], column_in_1.at[1], 2, 18),
        send_near(column_pay_1.at[1], column_in_1.at[0], 3, 19),
    ]

    for copy in margin_copies:
        copy.wait_recv()

    def widen(own, inbox):
        centre = [own[0:8], own[8:16], inbox(1)[0:8], inbox(0)[0:8]]
        right = [inbox(3)[0:8], inbox(3)[8:16], inbox(7)[0:8], inbox(5)[0:8]]
        left = [inbox(2)[0:8], inbox(2)[8:16], inbox(6)[0:8], inbox(4)[0:8]]
        return centre + [jnp.where(lane < 64, r, l) for r, l in zip(right, left)]

    def copy_sum(tiles):
        summed = []
        for side in range(2):
            part = tiles[4 * side : 4 * side + 4]
            prev = [pltpu.roll(v, 1, 0) for v in part]
            succ = [pltpu.roll(v, 7, 0) for v in part]
            for i in range(4):
                before = jnp.where(sub == 0, prev[i - 1], prev[i])
                after = jnp.where(sub == 7, succ[(i + 1) % 4], succ[i])
                summed.append(
                    part[i] + jnp.where(first_x, before, 0.0) + jnp.where(last_x, after, 0.0)
                )
        prev = [pltpu.roll(v, 1, 1) for v in summed]
        succ = [pltpu.roll(v, 127, 1) for v in summed]
        result = []
        for i in range(8):
            other = (i + 4) % 8
            before = jnp.where(lane == 0, prev[other], prev[i])
            after = jnp.where(lane == 127, succ[other], succ[i])
            result.append(
                summed[i] + jnp.where(first_y, before, 0.0) + jnp.where(last_y, after, 0.0)
            )
        return result

    taps_x = [(s, tap_table(x_pos, s)) for s in shifts]
    centre_x = tap_table(x_pos, 0)

    def without_surface(v, wind_x, wind_y):
        slope_x = centre_x * v
        for s, tap in taps_x:
            slope_x = slope_x + tap * pltpu.roll(v, (-s) % 8, 0)
        return v - F32(TIME_STEP) * (wind_x * slope_x + wind_y * slope_y(v)) - F32(RELAX) * v

    wide = [
        widen(margin_pay[q], lambda d, q=q: margin_in[d, q]) for q in range(4)
    ]
    wide_mass = [gll_weight * v for v in wide[3]]
    wide_inverse = [1.0 / v for v in copy_sum(wide_mass)]
    for i in range(8):
        base_ref[i] = without_surface(wide[0][i], wide[1][i], wide[2][i])
        wide_ref[0, i] = wide[1][i]
        wide_ref[1, i] = wide[2][i]
        wide_ref[2, i] = wide_mass[i]
        wide_ref[3, i] = wide_inverse[i]
    for half in range(2):
        inverse_ref[8 * half : 8 * half + 8, :] = wide_inverse[half]

    for copy in column_copies:
        copy.wait_recv()

    def keep(g, x, v):
        field_1[x, pl.ds(pl.multiple_of(g * 8, 8), 8), :] = v

    sum_columns(column_in_1, keep)
    advance(lambda g, x: field_1[x, pl.ds(pl.multiple_of(g * 8, 8), 8), :], weighted_2)
    row_copies = [
        send_near(weighted_2.at[1], weighted_2.at[17], 0, 20),
        send_near(weighted_2.at[16], weighted_2.at[0], 1, 21),
    ]

    await_all(heat_in, all_recv.at[0])
    build_left(
        rows_ref,
        lambda base: (heat_in[pl.ds(base, 8), 0, :], heat_in[pl.ds(base, 8), 1, :]),
        left_ref,
    )
    heat, frac = scatter_sums(left_ref, hot_rows, 2)
    surf_pay[...] = (heat + land_ref[...] * air_ref[0:16, :]) / (frac + land_ref[...])
    for d in range(8):
        low, high = MARGIN_ROWS[DIRECTIONS[d][0]]
        surf_copies.append(
            send_near(
                surf_pay.at[low:high, :],
                surf_in.at[REVERSE[d], 0 : high - low, :],
                d,
                8 + d,
            )
        )

    for copy in row_copies:
        copy.wait_recv()
    sum_rows(weighted_2, column_pay_2)
    column_copies = [
        send_near(column_pay_2.at[0], column_in_2.at[1], 2, 22),
        send_near(column_pay_2.at[1], column_in_2.at[0], 3, 23),
    ]

    for copy in surf_copies:
        copy.wait_recv()
    surf = widen(surf_pay[...], lambda d: surf_in[d])
    moved = [
        wide_ref[2, i] * (base_ref[i] + F32(RELAX) * surf[i]) for i in range(8)
    ]
    field = [v * wide_ref[3, i] for i, v in enumerate(copy_sum(moved))]
    moved = [
        wide_ref[2, i]
        * (without_surface(field[i], wide_ref[0, i], wide_ref[1, i]) + F32(RELAX) * surf[i])
        for i in range(8)
    ]
    final = [v * wide_ref[3, i] for i, v in enumerate(copy_sum(moved)[0:2])]
    flux = [
        jnp.broadcast_to((final[h // 8] - surf[h // 8])[h % 8 : h % 8 + 1], TILE)
        for h in range(16)
    ]
    for i in range(n_blk // 8):
        idx = rows_ref[8 * i : 8 * i + 8, :]
        flux_pay[8 * i : 8 * i + 8, 0, :] = lane_gather(
            flux, lax.shift_right_logical(idx, 7), lax.bitwise_and(idx, 127)
        )
    exchange(flux_pay, flux_in, 1)
    flux_in[blk] = flux_pay[blk]

    for copy in column_copies:
        copy.wait_recv()

    def put_out(g, x, v):
        air_out[pl.ds(g * 128 + x, 8, stride=16), :] = v

    sum_columns(column_in_2, put_out)
    for half in range(2):
        air_out[8 * half : 8 * half + 8, :] = final[half]
    build_hot(cols_ref, hot_cols)
    for copy in rim_copies:
        copy.wait_recv()
    ocean(0, 16)

    await_all(flux_in, all_recv.at[1])
    build_left(
        cols_ref,
        lambda base: (weight_ref[pl.ds(base, 8), :] * flux_in[pl.ds(base, 8), 0, :],),
        left_ref,
    )
    (inflow,) = scatter_sums(left_ref, hot_cols, 1)
    gain = F32(FLUX_GAIN) * inflow / area_ref[...]
    for h in range(16):
        here = slice(128 * h, 128 * h + 128)
        ocean_out[0:1, here] = ocean_out[0:1, here] + gain[h : h + 1]

    for copy in started:
        copy.wait_send()
    await_all(heat_pay, all_send.at[0])
    await_all(flux_pay, all_send.at[1])


def solution(mesh):
    n_face, n_blk = mesh.shape["face"], mesh.shape["blk"]

    def body(
        air_state,
        air_wind,
        jacobian,
        land_area,
        xgrid_rows,
        tracers,
        edge_coef,
        neighbours,
        vert_rate,
        ocean_area,
        send_list,
        xgrid_cols,
        xgrid_weights,
    ):
        air_shape, ocean_shape = air_state.shape, tracers.shape
        vmem = pltpu.VMEM
        air, ocean = pl.pallas_call(
            lambda *refs: interval_kernel(n_face, n_blk, *refs),
            out_shape=(
                jax.ShapeDtypeStruct((768, 128), F32),
                jax.ShapeDtypeStruct((32, 2048), F32),
            ),
            in_specs=[pl.BlockSpec(memory_space=vmem)] * 13,
            out_specs=(pl.BlockSpec(memory_space=vmem),) * 2,
            scratch_shapes=[
                vmem((n_blk, 2, 128), F32),
                vmem((n_blk, 2, 128), F32),
                vmem((n_blk, 1, 128), F32),
                vmem((n_blk, 1, 128), F32),
                vmem((2, 32, 128), F32),
                vmem((2, 32, 128), F32),
                vmem((4, 16, 128), F32),
                vmem((8, 4, 16, 128), F32),
                vmem((16, 128), F32),
                vmem((8, 16, 128), F32),
                vmem((18, 48, 128), F32),
                vmem((18, 48, 128), F32),
                vmem((16, 48, 128), F32),
                vmem((2, 48, 128), F32),
                vmem((2, 48, 128), F32),
                vmem((2, 48, 128), F32),
                vmem((2, 48, 128), F32),
                vmem((16, 48, 128), F32),
                vmem((16, 128), F32),
                vmem((16, 128), F32),
                vmem((128, 128 * n_blk), BF16),
                vmem((128, 128 * n_blk), BF16),
                vmem((96, 128 * n_blk), BF16),
                vmem((8, 8, 128), F32),
                vmem((4, 8, 8, 128), F32),
                pltpu.SemaphoreType.DMA((2,)),
                pltpu.SemaphoreType.DMA((2,)),
                pltpu.SemaphoreType.DMA((26,)),
                pltpu.SemaphoreType.DMA((26,)),
            ],
            compiler_params=pltpu.CompilerParams(collective_id=0, has_side_effects=True),
            name="interval",
        )(
            air_state.reshape(768, 128),
            air_wind.reshape(512, 128),
            jacobian,
            land_area,
            xgrid_rows[0],
            tracers.reshape(32, 2048),
            edge_coef,
            neighbours,
            vert_rate.reshape(16, 128),
            ocean_area.reshape(16, 128),
            send_list.reshape(2, 128),
            xgrid_cols[0],
            xgrid_weights[0],
        )
        return air.reshape(air_shape), ocean.reshape(ocean_shape)

    both = ("face", "blk")
    in_specs = (
        P(None, None, "face", "blk"),
        P(None, None, "face", "blk"),
        P("face", "blk"),
        P("face", "blk"),
        P(both, None, None),
        P(None, None, both),
        P(None, both),
        P(None, both),
        P(both),
        P(both),
        P(both, None),
        P(both, None, None),
        P(both, None, None),
    )
    out_specs = (P(None, None, "face", "blk"), P(None, None, both))
    return jax.shard_map(body, mesh=mesh, in_specs=in_specs, out_specs=out_specs, check_vma=False)
```

time: 414 us -> 59.6 us (0.14)
  the two profiles are of different devices: /device:TPU:1 before, /device:TPU:64 now
where the time goes in v2:
time: 59.6 us; the launch traced here: 59.4 us
  Pallas kernels  56.2 us (94%)
  local copies, waits for them, and re-layouts  2.52 us (4%)
  between operations  0.65 us (1%)
    pallas_call x1, Pallas kernels, body(): pl.pallas_call(lambda *refs: interval_kernel(n_face, n_blk, *refs), out_s...  56.2 us
    unnamed x4, local copies, waits for them, and re-layouts  2.52 us

profile of v2, /device:TPU:64, one launch (start us, length us, event | category | flops | bytes accessed | tf_op | source)
XLA Modules:
  0.0 59.4 jit_solution(7197869241955778906)
XLA Ops:
  0.6 56.2 %interval.1 = (f32[768,128]{1,0:T(8,128)}, f32[32,2048]{1,0:T(8,128)}) custom-call(f32[768,128]{1,0:T(8,128)} %bitcast.12, f32[512,128]{1,0:T(8,128)} %bitcast.14, f32[16,128]{1,0:T(8,128)} %refs_2_.1, f32[16,128]{1,0:T(8,128)} %refs_3_.1, s32[64,128]{1,0:T(8,128)} %bitcast.16, f32[32,2048]{1,0:T(8,128)} %bitcast.15, f32[6,2048]{1,0:T(8,128)} %refs_6_.1, ...), custom_call_target="tpu_custom_call" | custom-call | tf_op jit(solution)/shard_map/interval/pallas_call | solution.py:541
  56.9 0.0 copy-start
  56.9 1.8 %copy.17 = f32[3,16,16,128]{3,2,1,0:T(8,128)} copy(f32[3,16,16,128]{3,2,1,0:T(8,128)} %bitcast.11) | data formatting | bytes 786432
  58.7 0.0 copy-done
  58.7 0.7 %copy.18 = f32[2,16,2048]{2,1,0:T(8,128)} copy(f32[2,16,2048]{2,1,0:T(8,128)S(1)} %bitcast.13) | data formatting | bytes 524288
Async XLA Ops:
  56.9 1.8 %copy-start = (f32[32,2048]{1,0:T(8,128)S(1)}, f32[32,2048]{1,0:T(8,128)}, u32[]{:S(2)}) copy-start(f32[32,2048]{1,0:T(8,128)} %get-tuple-element.5) | copy-start | bytes 786436

commit v3 on v2

--- a/solution.py
+++ b/solution.py
@@ -95,6 +95,21 @@
 def interval_kernel(
     n_face,
     n_blk,
+    air_hbm,
+    wind_hbm,
+    jac_hbm,
+    land_hbm,
+    rows_hbm,
+    tracer_hbm,
+    coef_hbm,
+    near_hbm,
+    vert_hbm,
+    area_hbm,
+    send_hbm,
+    cols_hbm,
+    weight_hbm,
+    air_out,
+    ocean_out,
     air_ref,
     wind_ref,
     jac_ref,
@@ -108,8 +123,7 @@
     send_ref,
     cols_ref,
     weight_ref,
-    air_out,
-    ocean_out,
+    load_sem,
     heat_pay,
     heat_in,
     flux_pay,
@@ -146,16 +160,54 @@
         df, db = DIRECTIONS[d]
         return (lax.rem(face + df + n_face, n_face), lax.rem(blk + db + n_blk, n_blk))
 
+    names = (
+        *("cols", "weight", "tracer", "send", "air", "wind", "jac"),
+        *("rows", "land", "coef", "near", "vert", "area"),
+    )
+    pairs = {
+        "air": (air_hbm, air_ref),
+        "wind": (wind_hbm, wind_ref),
+        "jac": (jac_hbm, jac_ref),
+        "land": (land_hbm, land_ref),
+        "rows": (rows_hbm, rows_ref),
+        "tracer": (tracer_hbm, tracer_ref),
+        "coef": (coef_hbm, coef_ref),
+        "near": (near_hbm, near_ref),
+        "vert": (vert_hbm, vert_ref),
+        "area": (area_hbm, area_ref),
+        "send": (send_hbm, send_ref),
+        "cols": (cols_hbm, cols_ref),
+        "weight": (weight_hbm, weight_ref),
+    }
+    loads = {
+        name: pltpu.make_async_copy(*pairs[name], load_sem.at[i]) for i, name in enumerate(names)
+    }
+    for name in names:
+        loads[name].start()
+
+    def loaded(*wanted):
+        for name in wanted:
+            loads[name].wait()
+
+    def every_peer(act):
+        half = n_blk // 2
+        act(lax.rem(blk + half, n_blk))
+
+        def both(k, carry):
+            act(lax.rem(blk + half + k, n_blk))
+            act(lax.rem(blk + half - k, n_blk))
+            return carry
+
+        lax.fori_loop(1, half, both, 0)
+
     barrier = pltpu.get_barrier_semaphore()
-
-    def greet(k, carry):
-        peer = lax.rem(blk + k, n_blk)
-        pl.semaphore_signal(barrier, inc=1, device_id=(face, peer), device_id_type=MESH)
-        return carry
-
-    lax.fori_loop(1, n_blk, greet, 0)
-    for d in (0, 1, 4, 5, 6, 7):
+    for d in (4, 5, 6, 7, 0, 1):
         pl.semaphore_signal(barrier, inc=1, device_id=step_to(d), device_id_type=MESH)
+    every_peer(
+        lambda peer: pl.semaphore_signal(
+            barrier, inc=1, device_id=(face, peer), device_id_type=MESH
+        )
+    )
 
     sub = lax.broadcasted_iota(jnp.int32, TILE, 0)
     lane = lax.broadcasted_iota(jnp.int32, TILE, 1)
@@ -168,6 +220,7 @@
     )
     shifts = (-3, -2, -1, 1, 2, 3)
 
+    loaded("cols", "weight", "tracer")
     surface = [
         jnp.broadcast_to(tracer_ref[0:1, 128 * h : 128 * h + 128], TILE) for h in range(16)
     ]
@@ -178,6 +231,63 @@
         heat_pay[8 * i : 8 * i + 8, 0, :] = weight * at
         heat_pay[8 * i : 8 * i + 8, 1, :] = weight
 
+    pl.semaphore_wait(barrier, n_blk - 1 + 6)
+
+    def exchange(pay, inbox, slot):
+        every_peer(
+            lambda peer: pltpu.make_async_remote_copy(
+                src_ref=pay.at[peer],
+                dst_ref=inbox.at[blk],
+                send_sem=all_send.at[slot],
+                recv_sem=all_recv.at[slot],
+                device_id=(face, peer),
+                device_id_type=MESH,
+            ).start()
+        )
+
+    def await_all(ref, sem):
+        rest = ref.at[pl.ds(0, n_blk - 1)]
+        pltpu.make_async_copy(rest, rest, sem).wait()
+
+    started = []
+
+    def send_near(src, dst, d, slot):
+        copy = pltpu.make_async_remote_copy(
+            src_ref=src,
+            dst_ref=dst,
+            send_sem=near_send.at[slot],
+            recv_sem=near_recv.at[slot],
+            device_id=step_to(d),
+            device_id_type=MESH,
+        )
+        copy.start()
+        started.append(copy)
+        return copy
+
+    exchange(heat_pay, heat_in, 0)
+    heat_in[blk] = heat_pay[blk]
+
+    loaded("air", "wind", "jac")
+    margin_pay[0] = air_ref[0:16, :]
+    margin_pay[1] = wind_ref[0:16, :]
+    margin_pay[2] = wind_ref[256:272, :]
+    margin_pay[3] = jac_ref[...]
+    for half in range(2):
+        mass_ref[8 * half : 8 * half + 8, :] = gll_weight * jac_ref[8 * half : 8 * half + 8, :]
+
+    margin_copies, surf_copies = [], []
+    for d in range(8):
+        low, high = MARGIN_ROWS[DIRECTIONS[d][0]]
+        margin_copies.append(
+            send_near(
+                margin_pay.at[:, low:high, :],
+                margin_in.at[REVERSE[d], :, 0 : high - low, :],
+                d,
+                d,
+            )
+        )
+
+    loaded("send")
     for side in range(2):
         idx = jnp.broadcast_to(send_ref[side : side + 1, :], TILE)
         hi, lo = lax.shift_right_logical(idx, 7), lax.bitwise_and(idx, 127)
@@ -185,12 +295,10 @@
             tiles = [tracer_ref[8 * g : 8 * g + 8, 128 * h : 128 * h + 128] for h in range(16)]
             rim_pay[side, 8 * g : 8 * g + 8, :] = lane_gather(tiles, hi, lo)
 
-    margin_pay[0] = air_ref[0:16, :]
-    margin_pay[1] = wind_ref[0:16, :]
-    margin_pay[2] = wind_ref[256:272, :]
-    margin_pay[3] = jac_ref[...]
-    for half in range(2):
-        mass_ref[8 * half : 8 * half + 8, :] = gll_weight * jac_ref[8 * half : 8 * half + 8, :]
+    rim_copies = [
+        send_near(rim_pay.at[0], rim_in.at[1], 2, 24),
+        send_near(rim_pay.at[1], rim_in.at[0], 3, 25),
+    ]
 
     taps_y = [(s, tap_table(y_pos, s)) for s in shifts]
     centre_y = tap_table(y_pos, 0)
@@ -225,65 +333,12 @@
         lax.fori_loop(0, 6, group, 0)
 
     advance(lambda g, x: air_ref[pl.ds(g * 128 + x, 8, stride=16), :], weighted_1)
-    build_hot(rows_ref, hot_rows)
-
-    pl.semaphore_wait(barrier, n_blk - 1 + 6)
-
-    def exchange(pay, inbox, slot):
-        def send(k, carry):
-            peer = lax.rem(blk + k, n_blk)
-            pltpu.make_async_remote_copy(
-                src_ref=pay.at[peer],
-                dst_ref=inbox.at[blk],
-                send_sem=all_send.at[slot],
-                recv_sem=all_recv.at[slot],
-                device_id=(face, peer),
-                device_id_type=MESH,
-            ).start()
-            return carry
-
-        lax.fori_loop(1, n_blk, send, 0)
-
-    def await_all(ref, sem):
-        rest = ref.at[pl.ds(0, n_blk - 1)]
-        pltpu.make_async_copy(rest, rest, sem).wait()
-
-    started = []
-
-    def send_near(src, dst, d, slot):
-        copy = pltpu.make_async_remote_copy(
-            src_ref=src,
-            dst_ref=dst,
-            send_sem=near_send.at[slot],
-            recv_sem=near_recv.at[slot],
-            device_id=step_to(d),
-            device_id_type=MESH,
-        )
-        copy.start()
-        started.append(copy)
-        return copy
-
-    exchange(heat_pay, heat_in, 0)
-    margin_copies, surf_copies = [], []
-    for d in range(8):
-        low, high = MARGIN_ROWS[DIRECTIONS[d][0]]
-        margin_copies.append(
-            send_near(
-                margin_pay.at[:, low:high, :],
-                margin_in.at[REVERSE[d], :, 0 : high - low, :],
-                d,
-                d,
-            )
-        )
     row_copies = [
         send_near(weighted_1.at[1], weighted_1.at[17], 0, 16),
         send_near(weighted_1.at[16], weighted_1.at[0], 1, 17),
     ]
-    rim_copies = [
-        send_near(rim_pay.at[0], rim_in.at[1], 2, 24),
-        send_near(rim_pay.at[1], rim_in.at[0], 3, 25),
-    ]
-    heat_in[blk] = heat_pay[blk]
+    loaded("rows", "land", "coef", "near", "vert", "area")
+    build_hot(rows_ref, hot_rows)
 
     def ocean(first, last):
         def block(j, carry):
@@ -434,6 +489,19 @@
         send_near(weighted_2.at[16], weighted_2.at[0], 1, 21),
     ]
 
+    build_hot(cols_ref, hot_cols)
+    for copy in rim_copies:
+        copy.wait_recv()
+    ocean(0, 2)
+    for copy in row_copies:
+        copy.wait_recv()
+    sum_rows(weighted_2, column_pay_2)
+    column_copies = [
+        send_near(column_pay_2.at[0], column_in_2.at[1], 2, 22),
+        send_near(column_pay_2.at[1], column_in_2.at[0], 3, 23),
+    ]
+    ocean(2, 4)
+
     await_all(heat_in, all_recv.at[0])
     build_left(
         rows_ref,
@@ -453,13 +521,14 @@
             )
         )
 
-    for copy in row_copies:
+    for copy in column_copies:
         copy.wait_recv()
-    sum_rows(weighted_2, column_pay_2)
-    column_copies = [
-        send_near(column_pay_2.at[0], column_in_2.at[1], 2, 22),
-        send_near(column_pay_2.at[1], column_in_2.at[0], 3, 23),
-    ]
+
+    def put_out(g, x, v):
+        air_out[pl.ds(g * 128 + x, 8, stride=16), :] = v
+
+    sum_columns(column_in_2, put_out)
+    ocean(4, 7)
 
     for copy in surf_copies:
         copy.wait_recv()
@@ -486,19 +555,9 @@
     exchange(flux_pay, flux_in, 1)
     flux_in[blk] = flux_pay[blk]
 
-    for copy in column_copies:
-        copy.wait_recv()
-
-    def put_out(g, x, v):
-        air_out[pl.ds(g * 128 + x, 8, stride=16), :] = v
-
-    sum_columns(column_in_2, put_out)
     for half in range(2):
         air_out[8 * half : 8 * half + 8, :] = final[half]
-    build_hot(cols_ref, hot_cols)
-    for copy in rim_copies:
-        copy.wait_recv()
-    ocean(0, 16)
+    ocean(7, 16)
 
     await_all(flux_in, all_recv.at[1])
     build_left(
@@ -540,13 +599,24 @@
         vmem = pltpu.VMEM
         air, ocean = pl.pallas_call(
             lambda *refs: interval_kernel(n_face, n_blk, *refs),
-            out_shape=(
-                jax.ShapeDtypeStruct((768, 128), F32),
-                jax.ShapeDtypeStruct((32, 2048), F32),
-            ),
-            in_specs=[pl.BlockSpec(memory_space=vmem)] * 13,
+            out_shape=(vmem((768, 128), F32), vmem((32, 2048), F32)),
+            in_specs=[pl.BlockSpec(memory_space=pl.ANY)] * 13,
             out_specs=(pl.BlockSpec(memory_space=vmem),) * 2,
             scratch_shapes=[
+                vmem((768, 128), F32),
+                vmem((512, 128), F32),
+                vmem((16, 128), F32),
+                vmem((16, 128), F32),
+                vmem((n_blk, 128), jnp.int32),
+                vmem((32, 2048), F32),
+                vmem((6, 2048), F32),
+                vmem((6, 2048), jnp.int32),
+                vmem((16, 128), F32),
+                vmem((16, 128), F32),
+                vmem((2, 128), jnp.int32),
+                vmem((n_blk, 128), jnp.int32),
+                vmem((n_blk, 128), F32),
+                pltpu.SemaphoreType.DMA((13,)),
                 vmem((n_blk, 2, 128), F32),
                 vmem((n_blk, 2, 128), F32),
                 vmem((n_blk, 1, 128), F32),

time: 59.6 us -> 55.3 us (0.928)
  the two profiles are of different devices: /device:TPU:64 before, /device:TPU:1 now
where the time goes in v3:
time: 55.3 us; the launch traced here: 55.1 us
  Pallas kernels  53 us (96%)
  local copies, waits for them, and re-layouts  1.45 us (3%)
  between operations  0.64 us (1%)
    pallas_call x1, Pallas kernels, body(): pl.pallas_call(lambda *refs: interval_kernel(n_face, n_blk, *refs), out_s...  53 us
    unnamed x2, local copies, waits for them, and re-layouts  1.45 us

profile of v3, /device:TPU:1, one launch (start us, length us, event | category | flops | bytes accessed | tf_op | source)
XLA Modules:
  0.0 55.1 jit_solution(17693878684096779347)
XLA Ops:
  0.6 53.0 %interval.1 = (f32[768,128]{1,0:T(8,128)S(1)}, f32[32,2048]{1,0:T(8,128)S(1)}) custom-call(f32[768,128]{1,0:T(8,128)} %bitcast.13, f32[512,128]{1,0:T(8,128)} %bitcast.14, f32[16,128]{1,0:T(8,128)} %refs_2_.1, f32[16,128]{1,0:T(8,128)} %refs_3_.1, s32[64,128]{1,0:T(8,128)} %bitcast.16, f32[32,2048]{1,0:T(8,128)} %bitcast.15, f32[6,2048]{1,0:T(8,128)} %refs_6_.1, ...), custom_call_target="tpu_custom_call" | custom-call | tf_op jit(solution)/shard_map/interval/pallas_call | solution.py:600
  53.7 0.7 %copy.17 = f32[3,16,16,128]{3,2,1,0:T(8,128)} copy(f32[3,16,16,128]{3,2,1,0:T(8,128)S(1)} %bitcast.11) | data formatting | bytes 786432
  54.4 0.7 %copy.18 = f32[2,16,2048]{2,1,0:T(8,128)} copy(f32[2,16,2048]{2,1,0:T(8,128)S(1)} %bitcast.12) | data formatting | bytes 524288

commit v4 on v3

--- a/solution.py
+++ b/solution.py
@@ -22,6 +22,7 @@
 F32 = jnp.float32
 BF16 = jnp.bfloat16
 TILE = (8, 128)
+PARTS = 2
 
 
 def lane_gather(rows, hi, lo):
@@ -61,7 +62,7 @@
         hi = lax.shift_right_logical(idx_ref[pl.ds(base, 8), :], 7)
         parts = []
         for rest in values_at(base):
-            for _ in range(3):
+            for _ in range(PARTS):
                 part = rest.astype(BF16).astype(F32)
                 parts.append(part)
                 rest = rest - part
@@ -80,14 +81,15 @@
 
 
 def scatter_sums(left_ref, hot_ref, count):
+    size = 16 * PARTS
     total = lax.dot_general(
-        left_ref[0 : 48 * count, :],
+        left_ref[0 : size * count, :],
         hot_ref[...],
         (((1,), (1,)), ((), ())),
         preferred_element_type=F32,
     )
     return [
-        total[48 * q : 48 * q + 16] + total[48 * q + 16 : 48 * q + 32] + total[48 * q + 32 : 48 * q + 48]
+        sum(total[size * q + 16 * p : size * q + 16 * p + 16] for p in range(PARTS))
         for q in range(count)
     ]
 
@@ -412,6 +414,9 @@
 
         lax.fori_loop(0, 6, group, 0)
 
+    for copy in rim_copies:
+        copy.wait_recv()
+    ocean(0, 3)
     for copy in row_copies:
         copy.wait_recv()
     sum_rows(weighted_1, column_pay_1)
@@ -476,6 +481,7 @@
     for half in range(2):
         inverse_ref[8 * half : 8 * half + 8, :] = wide_inverse[half]
 
+    ocean(3, 6)
     for copy in column_copies:
         copy.wait_recv()
 
@@ -490,17 +496,6 @@
     ]
 
     build_hot(cols_ref, hot_cols)
-    for copy in rim_copies:
-        copy.wait_recv()
-    ocean(0, 2)
-    for copy in row_copies:
-        copy.wait_recv()
-    sum_rows(weighted_2, column_pay_2)
-    column_copies = [
-        send_near(column_pay_2.at[0], column_in_2.at[1], 2, 22),
-        send_near(column_pay_2.at[1], column_in_2.at[0], 3, 23),
-    ]
-    ocean(2, 4)
 
     await_all(heat_in, all_recv.at[0])
     build_left(
@@ -521,14 +516,14 @@
             )
         )
 
-    for copy in column_copies:
+    for copy in row_copies:
         copy.wait_recv()
-
-    def put_out(g, x, v):
-        air_out[pl.ds(g * 128 + x, 8, stride=16), :] = v
-
-    sum_columns(column_in_2, put_out)
-    ocean(4, 7)
+    sum_rows(weighted_2, column_pay_2)
+    column_copies = [
+        send_near(column_pay_2.at[0], column_in_2.at[1], 2, 22),
+        send_near(column_pay_2.at[1], column_in_2.at[0], 3, 23),
+    ]
+    ocean(6, 9)
 
     for copy in surf_copies:
         copy.wait_recv()
@@ -555,9 +550,16 @@
     exchange(flux_pay, flux_in, 1)
     flux_in[blk] = flux_pay[blk]
 
+    for copy in column_copies:
+        copy.wait_recv()
+
+    def put_out(g, x, v):
+        air_out[pl.ds(g * 128 + x, 8, stride=16), :] = v
+
+    sum_columns(column_in_2, put_out)
     for half in range(2):
         air_out[8 * half : 8 * half + 8, :] = final[half]
-    ocean(7, 16)
+    ocean(9, 16)
 
     await_all(flux_in, all_recv.at[1])
     build_left(
@@ -639,7 +641,7 @@
                 vmem((16, 128), F32),
                 vmem((128, 128 * n_blk), BF16),
                 vmem((128, 128 * n_blk), BF16),
-                vmem((96, 128 * n_blk), BF16),
+                vmem((32 * PARTS, 128 * n_blk), BF16),
                 vmem((8, 8, 128), F32),
                 vmem((4, 8, 8, 128), F32),
                 pltpu.SemaphoreType.DMA((2,)),

time: 55.3 us -> 55.1 us (level)
  no operation moved by 1% of the time
where the time goes in v4:
time: 55.1 us; the launch traced here: 55 us
  Pallas kernels  52.9 us (96%)
  local copies, waits for them, and re-layouts  1.45 us (3%)
  between operations  0.64 us (1%)
    pallas_call x1, Pallas kernels, body(): pl.pallas_call(lambda *refs: interval_kernel(n_face, n_blk, *refs), out_s...  52.9 us
    unnamed x2, local copies, waits for them, and re-layouts  1.45 us

profile of v4, /device:TPU:1, one launch (start us, length us, event | category | flops | bytes accessed | tf_op | source)
XLA Modules:
  0.0 55.0 jit_solution(12455429732477511059)
XLA Ops:
  0.6 52.9 %interval.1 = (f32[768,128]{1,0:T(8,128)S(1)}, f32[32,2048]{1,0:T(8,128)S(1)}) custom-call(f32[768,128]{1,0:T(8,128)} %bitcast.13, f32[512,128]{1,0:T(8,128)} %bitcast.14, f32[16,128]{1,0:T(8,128)} %refs_2_.1, f32[16,128]{1,0:T(8,128)} %refs_3_.1, s32[64,128]{1,0:T(8,128)} %bitcast.16, f32[32,2048]{1,0:T(8,128)} %bitcast.15, f32[6,2048]{1,0:T(8,128)} %refs_6_.1, ...), custom_call_target="tpu_custom_call" | custom-call | tf_op jit(solution)/shard_map/interval/pallas_call | solution.py:602
  53.5 0.7 %copy.17 = f32[3,16,16,128]{3,2,1,0:T(8,128)} copy(f32[3,16,16,128]{3,2,1,0:T(8,128)S(1)} %bitcast.11) | data formatting | bytes 786432
  54.3 0.7 %copy.18 = f32[2,16,2048]{2,1,0:T(8,128)} copy(f32[2,16,2048]{2,1,0:T(8,128)S(1)} %bitcast.12) | data formatting | bytes 524288

commit v5 on v4

--- a/solution.py
+++ b/solution.py
@@ -23,6 +23,7 @@
 BF16 = jnp.bfloat16
 TILE = (8, 128)
 PARTS = 2
+EARLY = 5
 
 
 def lane_gather(rows, hi, lo):
@@ -233,42 +234,6 @@
         heat_pay[8 * i : 8 * i + 8, 0, :] = weight * at
         heat_pay[8 * i : 8 * i + 8, 1, :] = weight
 
-    pl.semaphore_wait(barrier, n_blk - 1 + 6)
-
-    def exchange(pay, inbox, slot):
-        every_peer(
-            lambda peer: pltpu.make_async_remote_copy(
-                src_ref=pay.at[peer],
-                dst_ref=inbox.at[blk],
-                send_sem=all_send.at[slot],
-                recv_sem=all_recv.at[slot],
-                device_id=(face, peer),
-                device_id_type=MESH,
-            ).start()
-        )
-
-    def await_all(ref, sem):
-        rest = ref.at[pl.ds(0, n_blk - 1)]
-        pltpu.make_async_copy(rest, rest, sem).wait()
-
-    started = []
-
-    def send_near(src, dst, d, slot):
-        copy = pltpu.make_async_remote_copy(
-            src_ref=src,
-            dst_ref=dst,
-            send_sem=near_send.at[slot],
-            recv_sem=near_recv.at[slot],
-            device_id=step_to(d),
-            device_id_type=MESH,
-        )
-        copy.start()
-        started.append(copy)
-        return copy
-
-    exchange(heat_pay, heat_in, 0)
-    heat_in[blk] = heat_pay[blk]
-
     loaded("air", "wind", "jac")
     margin_pay[0] = air_ref[0:16, :]
     margin_pay[1] = wind_ref[0:16, :]
@@ -277,18 +242,6 @@
     for half in range(2):
         mass_ref[8 * half : 8 * half + 8, :] = gll_weight * jac_ref[8 * half : 8 * half + 8, :]
 
-    margin_copies, surf_copies = [], []
-    for d in range(8):
-        low, high = MARGIN_ROWS[DIRECTIONS[d][0]]
-        margin_copies.append(
-            send_near(
-                margin_pay.at[:, low:high, :],
-                margin_in.at[REVERSE[d], :, 0 : high - low, :],
-                d,
-                d,
-            )
-        )
-
     loaded("send")
     for side in range(2):
         idx = jnp.broadcast_to(send_ref[side : side + 1, :], TILE)
@@ -296,11 +249,6 @@
         for g in range(4):
             tiles = [tracer_ref[8 * g : 8 * g + 8, 128 * h : 128 * h + 128] for h in range(16)]
             rim_pay[side, 8 * g : 8 * g + 8, :] = lane_gather(tiles, hi, lo)
-
-    rim_copies = [
-        send_near(rim_pay.at[0], rim_in.at[1], 2, 24),
-        send_near(rim_pay.at[1], rim_in.at[0], 3, 25),
-    ]
 
     taps_y = [(s, tap_table(y_pos, s)) for s in shifts]
     centre_y = tap_table(y_pos, 0)
@@ -335,14 +283,67 @@
         lax.fori_loop(0, 6, group, 0)
 
     advance(lambda g, x: air_ref[pl.ds(g * 128 + x, 8, stride=16), :], weighted_1)
+    loaded("rows", "land", "coef", "near", "vert", "area")
+    build_hot(rows_ref, hot_rows)
+
+    pl.semaphore_wait(barrier, n_blk - 1 + 6)
+
+    def exchange(pay, inbox, slot):
+        every_peer(
+            lambda peer: pltpu.make_async_remote_copy(
+                src_ref=pay.at[peer],
+                dst_ref=inbox.at[blk],
+                send_sem=all_send.at[slot],
+                recv_sem=all_recv.at[slot],
+                device_id=(face, peer),
+                device_id_type=MESH,
+            ).start()
+        )
+
+    def await_all(ref, sem):
+        rest = ref.at[pl.ds(0, n_blk - 1)]
+        pltpu.make_async_copy(rest, rest, sem).wait()
+
+    started = []
+
+    def send_near(src, dst, d, slot):
+        copy = pltpu.make_async_remote_copy(
+            src_ref=src,
+            dst_ref=dst,
+            send_sem=near_send.at[slot],
+            recv_sem=near_recv.at[slot],
+            device_id=step_to(d),
+            device_id_type=MESH,
+        )
+        copy.start()
+        started.append(copy)
+        return copy
+
+    exchange(heat_pay, heat_in, 0)
+    heat_in[blk] = heat_pay[blk]
+
+    margin_copies, surf_copies = [], []
+    for d in range(8):
+        low, high = MARGIN_ROWS[DIRECTIONS[d][0]]
+        margin_copies.append(
+            send_near(
+                margin_pay.at[:, low:high, :],
+                margin_in.at[REVERSE[d], :, 0 : high - low, :],
+                d,
+                d,
+            )
+        )
+
+    rim_copies = [
+        send_near(rim_pay.at[0], rim_in.at[1], 2, 24),
+        send_near(rim_pay.at[1], rim_in.at[0], 3, 25),
+    ]
+
     row_copies = [
         send_near(weighted_1.at[1], weighted_1.at[17], 0, 16),
         send_near(weighted_1.at[16], weighted_1.at[0], 1, 17),
     ]
-    loaded("rows", "land", "coef", "near", "vert", "area")
-    build_hot(rows_ref, hot_rows)
-
-    def ocean(first, last):
+    def ocean(first, last, tables=18):
         def block(j, carry):
             here = pl.ds(pl.multiple_of(j * 128, 128), 128)
             own = [tracer_ref[8 * g : 8 * g + 8, here] for g in range(4)]
@@ -352,7 +353,7 @@
                 coef = jnp.broadcast_to(coef_ref[e : e + 1, here], TILE)
                 hi, lo = lax.shift_right_logical(idx, 7), lax.bitwise_and(idx, 127)
                 found = [jnp.zeros(TILE, F32) for g in range(4)]
-                for h in range(18):
+                for h in range(tables):
                     mine = hi == h
                     for g in range(4):
                         if h < 16:
@@ -377,6 +378,28 @@
 
         lax.fori_loop(first, last, block, 0)
 
+    def ocean_rim(first, last):
+        def block(j, carry):
+            here = pl.ds(pl.multiple_of(j * 128, 128), 128)
+            lateral = [ocean_out[8 * g : 8 * g + 8, here] for g in range(4)]
+            for e in range(6):
+                idx = jnp.broadcast_to(near_ref[e : e + 1, here], TILE)
+                coef = jnp.broadcast_to(coef_ref[e : e + 1, here], TILE)
+                hi, lo = lax.shift_right_logical(idx, 7), lax.bitwise_and(idx, 127)
+                for g in range(4):
+                    found = jnp.zeros(TILE, F32)
+                    for side in range(2):
+                        tile = rim_in[side, 8 * g : 8 * g + 8, :]
+                        found = jnp.where(
+                            hi == 16 + side, jnp.take_along_axis(tile, lo, axis=1), found
+                        )
+                    lateral[g] = lateral[g] + coef * found
+            for g in range(4):
+                ocean_out[8 * g : 8 * g + 8, here] = lateral[g]
+            return carry
+
+        lax.fori_loop(first, last, block, 0)
+
     def sum_rows(weighted, column_pay):
         def group(g, carry):
             planes = pl.ds(pl.multiple_of(g * 8, 8), 8)
@@ -414,9 +437,8 @@
 
         lax.fori_loop(0, 6, group, 0)
 
-    for copy in rim_copies:
-        copy.wait_recv()
-    ocean(0, 3)
+    build_hot(cols_ref, hot_cols)
+    ocean(0, EARLY, 16)
     for copy in row_copies:
         copy.wait_recv()
     sum_rows(weighted_1, column_pay_1)
@@ -481,22 +503,6 @@
     for half in range(2):
         inverse_ref[8 * half : 8 * half + 8, :] = wide_inverse[half]
 
-    ocean(3, 6)
-    for copy in column_copies:
-        copy.wait_recv()
-
-    def keep(g, x, v):
-        field_1[x, pl.ds(pl.multiple_of(g * 8, 8), 8), :] = v
-
-    sum_columns(column_in_1, keep)
-    advance(lambda g, x: field_1[x, pl.ds(pl.multiple_of(g * 8, 8), 8), :], weighted_2)
-    row_copies = [
-        send_near(weighted_2.at[1], weighted_2.at[17], 0, 20),
-        send_near(weighted_2.at[16], weighted_2.at[0], 1, 21),
-    ]
-
-    build_hot(cols_ref, hot_cols)
-
     await_all(heat_in, all_recv.at[0])
     build_left(
         rows_ref,
@@ -516,14 +522,20 @@
             )
         )
 
-    for copy in row_copies:
+    for copy in column_copies:
         copy.wait_recv()
-    sum_rows(weighted_2, column_pay_2)
-    column_copies = [
-        send_near(column_pay_2.at[0], column_in_2.at[1], 2, 22),
-        send_near(column_pay_2.at[1], column_in_2.at[0], 3, 23),
-    ]
-    ocean(6, 9)
+
+    def keep(g, x, v):
+        field_1[x, pl.ds(pl.multiple_of(g * 8, 8), 8), :] = v
+
+    sum_columns(column_in_1, keep)
+    advance(lambda g, x: field_1[x, pl.ds(pl.multiple_of(g * 8, 8), 8), :], weighted_2)
+    row_copies = [
+        send_near(weighted_2.at[1], weighted_2.at[17], 0, 20),
+        send_near(weighted_2.at[16], weighted_2.at[0], 1, 21),
+    ]
+
+    ocean(EARLY, EARLY + 1, 16)
 
     for copy in surf_copies:
         copy.wait_recv()
@@ -550,6 +562,18 @@
     exchange(flux_pay, flux_in, 1)
     flux_in[blk] = flux_pay[blk]
 
+    for copy in rim_copies:
+        copy.wait_recv()
+    ocean(EARLY + 1, EARLY + 2)
+    for copy in row_copies:
+        copy.wait_recv()
+    sum_rows(weighted_2, column_pay_2)
+    column_copies = [
+        send_near(column_pay_2.at[0], column_in_2.at[1], 2, 22),
+        send_near(column_pay_2.at[1], column_in_2.at[0], 3, 23),
+    ]
+    ocean_rim(0, EARLY + 1)
+    ocean(EARLY + 2, 13)
     for copy in column_copies:
         copy.wait_recv()
 
@@ -559,7 +583,7 @@
     sum_columns(column_in_2, put_out)
     for half in range(2):
         air_out[8 * half : 8 * half + 8, :] = final[half]
-    ocean(9, 16)
+    ocean(13, 16)
 
     await_all(flux_in, all_recv.at[1])
     build_left(

time: 55.1 us -> 48.2 us (0.87)
  Pallas kernels: 52.9 us -> 46 us
    pallas_call x1, Pallas kernels: 52.9 us -> 46 us  [body(): pl.pallas_call(lambda *refs: interval_kernel(n_face, n_blk, *refs), out_s...]
where the time goes in v5:
time: 48.2 us; the launch traced here: 48 us
  Pallas kernels  46 us (95%)
  local copies, waits for them, and re-layouts  1.45 us (3%)
  between operations  0.64 us (1%)
    pallas_call x1, Pallas kernels, body(): pl.pallas_call(lambda *refs: interval_kernel(n_face, n_blk, *refs), out_s...  46 us
    unnamed x2, local copies, waits for them, and re-layouts  1.45 us

profile of v5, /device:TPU:1, one launch (start us, length us, event | category | flops | bytes accessed | tf_op | source)
XLA Modules:
  0.0 48.0 jit_solution(11555341841587965145)
XLA Ops:
  0.6 46.0 %interval.1 = (f32[768,128]{1,0:T(8,128)S(1)}, f32[32,2048]{1,0:T(8,128)S(1)}) custom-call(f32[768,128]{1,0:T(8,128)} %bitcast.13, f32[512,128]{1,0:T(8,128)} %bitcast.14, f32[16,128]{1,0:T(8,128)} %refs_2_.1, f32[16,128]{1,0:T(8,128)} %refs_3_.1, s32[64,128]{1,0:T(8,128)} %bitcast.16, f32[32,2048]{1,0:T(8,128)} %bitcast.15, f32[6,2048]{1,0:T(8,128)} %refs_6_.1, ...), custom_call_target="tpu_custom_call" | custom-call | tf_op jit(solution)/shard_map/interval/pallas_call | solution.py:626
  46.6 0.7 %copy.17 = f32[3,16,16,128]{3,2,1,0:T(8,128)} copy(f32[3,16,16,128]{3,2,1,0:T(8,128)S(1)} %bitcast.11) | data formatting | bytes 786432
  47.3 0.7 %copy.18 = f32[2,16,2048]{2,1,0:T(8,128)} copy(f32[2,16,2048]{2,1,0:T(8,128)S(1)} %bitcast.12) | data formatting | bytes 524288

commit v6 on v5

--- a/solution.py
+++ b/solution.py
@@ -107,12 +107,13 @@
     coef_hbm,
     near_hbm,
     vert_hbm,
-    area_hbm,
     send_hbm,
     cols_hbm,
     weight_hbm,
     air_out,
     ocean_out,
+    left_out,
+    hot_cols,
     air_ref,
     wind_ref,
     jac_ref,
@@ -122,7 +123,6 @@
     coef_ref,
     near_ref,
     vert_ref,
-    area_ref,
     send_ref,
     cols_ref,
     weight_ref,
@@ -148,7 +148,6 @@
     mass_ref,
     inverse_ref,
     hot_rows,
-    hot_cols,
     left_ref,
     base_ref,
     wide_ref,
@@ -165,7 +164,7 @@
 
     names = (
         *("cols", "weight", "tracer", "send", "air", "wind", "jac"),
-        *("rows", "land", "coef", "near", "vert", "area"),
+        *("rows", "land", "coef", "near", "vert"),
     )
     pairs = {
         "air": (air_hbm, air_ref),
@@ -177,7 +176,6 @@
         "coef": (coef_hbm, coef_ref),
         "near": (near_hbm, near_ref),
         "vert": (vert_hbm, vert_ref),
-        "area": (area_hbm, area_ref),
         "send": (send_hbm, send_ref),
         "cols": (cols_hbm, cols_ref),
         "weight": (weight_hbm, weight_ref),
@@ -283,7 +281,7 @@
         lax.fori_loop(0, 6, group, 0)
 
     advance(lambda g, x: air_ref[pl.ds(g * 128 + x, 8, stride=16), :], weighted_1)
-    loaded("rows", "land", "coef", "near", "vert", "area")
+    loaded("rows", "land", "coef", "near", "vert")
     build_hot(rows_ref, hot_rows)
 
     pl.semaphore_wait(barrier, n_blk - 1 + 6)
@@ -589,18 +587,32 @@
     build_left(
         cols_ref,
         lambda base: (weight_ref[pl.ds(base, 8), :] * flux_in[pl.ds(base, 8), 0, :],),
-        left_ref,
+        left_out,
     )
-    (inflow,) = scatter_sums(left_ref, hot_cols, 1)
-    gain = F32(FLUX_GAIN) * inflow / area_ref[...]
-    for h in range(16):
-        here = slice(128 * h, 128 * h + 128)
-        ocean_out[0:1, here] = ocean_out[0:1, here] + gain[h : h + 1]
-
     for copy in started:
         copy.wait_send()
     await_all(heat_pay, all_send.at[0])
     await_all(flux_pay, all_send.at[1])
+
+
+def finish_kernel(air_ref, ocean_ref, left_ref, hot_ref, area_ref, air_out, ocean_out, top, sem):
+    air_copy = pltpu.make_async_copy(air_ref, air_out, sem.at[0])
+    ocean_copy = pltpu.make_async_copy(
+        ocean_ref.at[pl.ds(8, 24), :], ocean_out.at[pl.ds(8, 24), :], sem.at[1]
+    )
+    air_copy.start()
+    ocean_copy.start()
+    (inflow,) = scatter_sums(left_ref, hot_ref, 1)
+    gain = F32(FLUX_GAIN) * inflow / area_ref[...]
+    first = lax.broadcasted_iota(jnp.int32, TILE, 0) == 0
+    for h in range(16):
+        here = slice(128 * h, 128 * h + 128)
+        add = jnp.where(first, jnp.broadcast_to(gain[h : h + 1], TILE), 0.0)
+        top[:, here] = ocean_ref[0:8, here] + add
+    top_copy = pltpu.make_async_copy(top, ocean_out.at[pl.ds(0, 8), :], sem.at[2])
+    top_copy.start()
+    for copy in (air_copy, ocean_copy, top_copy):
+        copy.wait()
 
 
 def solution(mesh):
@@ -623,11 +635,16 @@
     ):
         air_shape, ocean_shape = air_state.shape, tracers.shape
         vmem = pltpu.VMEM
-        air, ocean = pl.pallas_call(
+        air, ocean, left, hot = pl.pallas_call(
             lambda *refs: interval_kernel(n_face, n_blk, *refs),
-            out_shape=(vmem((768, 128), F32), vmem((32, 2048), F32)),
-            in_specs=[pl.BlockSpec(memory_space=pl.ANY)] * 13,
-            out_specs=(pl.BlockSpec(memory_space=vmem),) * 2,
+            out_shape=(
+                vmem((768, 128), F32),
+                vmem((32, 2048), F32),
+                vmem((16 * PARTS, 128 * n_blk), BF16),
+                vmem((128, 128 * n_blk), BF16),
+            ),
+            in_specs=[pl.BlockSpec(memory_space=pl.ANY)] * 12,
+            out_specs=(pl.BlockSpec(memory_space=vmem),) * 4,
             scratch_shapes=[
                 vmem((768, 128), F32),
                 vmem((512, 128), F32),
@@ -638,11 +655,10 @@
                 vmem((6, 2048), F32),
                 vmem((6, 2048), jnp.int32),
                 vmem((16, 128), F32),
-                vmem((16, 128), F32),
                 vmem((2, 128), jnp.int32),
                 vmem((n_blk, 128), jnp.int32),
                 vmem((n_blk, 128), F32),
-                pltpu.SemaphoreType.DMA((13,)),
+                pltpu.SemaphoreType.DMA((12,)),
                 vmem((n_blk, 2, 128), F32),
                 vmem((n_blk, 2, 128), F32),
                 vmem((n_blk, 1, 128), F32),
@@ -664,7 +680,6 @@
                 vmem((16, 128), F32),
                 vmem((16, 128), F32),
                 vmem((128, 128 * n_blk), BF16),
-                vmem((128, 128 * n_blk), BF16),
                 vmem((32 * PARTS, 128 * n_blk), BF16),
                 vmem((8, 8, 128), F32),
                 vmem((4, 8, 8, 128), F32),
@@ -685,11 +700,21 @@
             edge_coef,
             neighbours,
             vert_rate.reshape(16, 128),
-            ocean_area.reshape(16, 128),
             send_list.reshape(2, 128),
             xgrid_cols[0],
             xgrid_weights[0],
         )
+        air, ocean = pl.pallas_call(
+            finish_kernel,
+            out_shape=(
+                jax.ShapeDtypeStruct((768, 128), F32),
+                jax.ShapeDtypeStruct((32, 2048), F32),
+            ),
+            in_specs=[pl.BlockSpec(memory_space=vmem)] * 5,
+            out_specs=(pl.BlockSpec(memory_space=pl.ANY),) * 2,
+            scratch_shapes=[vmem((8, 2048), F32), pltpu.SemaphoreType.DMA((3,))],
+            name="finish",
+        )(*(pltpu.with_memory_space_constraint(v, vmem) for v in (air, ocean, left, hot)), ocean_area.reshape(16, 128))
         return air.reshape(air_shape), ocean.reshape(ocean_shape)
 
     both = ("face", "blk")

time: 48.2 us -> 47.8 us (level)
  local copies, waits for them, and re-layouts: 1.45 us -> 0 us
  Pallas kernels: 46 us -> 46.9 us
    pallas_call x0 -> x1, Pallas kernels: none -> 2.15 us  [body(): pl.pallas_call(finish_kernel, out_shape=(jax.ShapeDtypeStruct((768, 128),...]
    unnamed x2 -> x0, local copies, waits for them, and re-layouts: 1.45 us -> none
    pallas_call x1, Pallas kernels: 46 us -> 44.8 us  [body(): pl.pallas_call(lambda *refs: interval_kernel(n_face, n_blk, *refs), out_s...]
where the time goes in v6:
time: 47.8 us; the launch traced here: 47.6 us
  Pallas kernels  46.9 us (98%)
  between operations  0.64 us (1%)
    pallas_call x1, Pallas kernels, body(): pl.pallas_call(lambda *refs: interval_kernel(n_face, n_blk, *refs), out_s...  44.8 us
    pallas_call x1, Pallas kernels, body(): pl.pallas_call(finish_kernel, out_shape=(jax.ShapeDtypeStruct((768, 128),...  2.15 us

profile of v6, /device:TPU:1, one launch (start us, length us, event | category | flops | bytes accessed | tf_op | source)
XLA Modules:
  0.0 47.6 jit_solution(13390434951512265769)
XLA Ops:
  0.6 44.8 %interval.1 = (f32[768,128]{1,0:T(8,128)S(1)}, f32[32,2048]{1,0:T(8,128)S(1)}, bf16[32,8192]{1,0:T(8,128)(2,1)S(1)}, bf16[128,8192]{1,0:T(8,128)(2,1)S(1)}) custom-call(f32[768,128]{1,0:T(8,128)} %bitcast.11, f32[512,128]{1,0:T(8,128)} %bitcast.12, f32[16,128]{1,0:T(8,128)} %refs_2_.1, f32[16,128]{1,0:T(8,128)} %refs_3_.1, s32[64,128]{1,0:T(8,128)} %bitcast.14, ...), custom_call_target="tpu_custom_call" | custom-call | tf_op jit(solution)/shard_map/interval/pallas_call | solution.py:638
  45.4 2.1 %finish.1 = (f32[768,128]{1,0:T(8,128)}, f32[32,2048]{1,0:T(8,128)}) custom-call(f32[768,128]{1,0:T(8,128)S(1)} %get-tuple-element.8.air_ref, f32[32,2048]{1,0:T(8,128)S(1)} %get-tuple-element.9.ocean_ref, bf16[32,8192]{1,0:T(8,128)(2,1)S(1)} %get-tuple-element.10.left_ref, bf16[128,8192]{1,0:T(8,128)(2,1)S(1)} %get-tuple-element.11.hot_ref, f32[16,128]{1,0:T(8,128)} %bitcast.18), custom_call_target="tpu_custom_call" | custom-call | tf_op jit(solution)/shard_map/finish/pallas_call | solution.py:707

commit v7 on v6

--- a/solution.py
+++ b/solution.py
@@ -107,6 +107,7 @@
     coef_hbm,
     near_hbm,
     vert_hbm,
+    area_hbm,
     send_hbm,
     cols_hbm,
     weight_hbm,
@@ -114,6 +115,7 @@
     ocean_out,
     left_out,
     hot_cols,
+    area_out,
     air_ref,
     wind_ref,
     jac_ref,
@@ -164,7 +166,7 @@
 
     names = (
         *("cols", "weight", "tracer", "send", "air", "wind", "jac"),
-        *("rows", "land", "coef", "near", "vert"),
+        *("rows", "land", "coef", "near", "vert", "area"),
     )
     pairs = {
         "air": (air_hbm, air_ref),
@@ -176,6 +178,7 @@
         "coef": (coef_hbm, coef_ref),
         "near": (near_hbm, near_ref),
         "vert": (vert_hbm, vert_ref),
+        "area": (area_hbm, area_out),
         "send": (send_hbm, send_ref),
         "cols": (cols_hbm, cols_ref),
         "weight": (weight_hbm, weight_ref),
@@ -281,7 +284,7 @@
         lax.fori_loop(0, 6, group, 0)
 
     advance(lambda g, x: air_ref[pl.ds(g * 128 + x, 8, stride=16), :], weighted_1)
-    loaded("rows", "land", "coef", "near", "vert")
+    loaded("rows", "land", "coef", "near", "vert", "area")
     build_hot(rows_ref, hot_rows)
 
     pl.semaphore_wait(barrier, n_blk - 1 + 6)
@@ -635,16 +638,17 @@
     ):
         air_shape, ocean_shape = air_state.shape, tracers.shape
         vmem = pltpu.VMEM
-        air, ocean, left, hot = pl.pallas_call(
+        air, ocean, left, hot, area = pl.pallas_call(
             lambda *refs: interval_kernel(n_face, n_blk, *refs),
             out_shape=(
                 vmem((768, 128), F32),
                 vmem((32, 2048), F32),
                 vmem((16 * PARTS, 128 * n_blk), BF16),
                 vmem((128, 128 * n_blk), BF16),
+                vmem((16, 128), F32),
             ),
-            in_specs=[pl.BlockSpec(memory_space=pl.ANY)] * 12,
-            out_specs=(pl.BlockSpec(memory_space=vmem),) * 4,
+            in_specs=[pl.BlockSpec(memory_space=pl.ANY)] * 13,
+            out_specs=(pl.BlockSpec(memory_space=vmem),) * 5,
             scratch_shapes=[
                 vmem((768, 128), F32),
                 vmem((512, 128), F32),
@@ -658,7 +662,7 @@
                 vmem((2, 128), jnp.int32),
                 vmem((n_blk, 128), jnp.int32),
                 vmem((n_blk, 128), F32),
-                pltpu.SemaphoreType.DMA((12,)),
+                pltpu.SemaphoreType.DMA((13,)),
                 vmem((n_blk, 2, 128), F32),
                 vmem((n_blk, 2, 128), F32),
                 vmem((n_blk, 1, 128), F32),
@@ -700,6 +704,7 @@
             edge_coef,
             neighbours,
             vert_rate.reshape(16, 128),
+            ocean_area.reshape(16, 128),
             send_list.reshape(2, 128),
             xgrid_cols[0],
             xgrid_weights[0],
@@ -714,7 +719,7 @@
             out_specs=(pl.BlockSpec(memory_space=pl.ANY),) * 2,
             scratch_shapes=[vmem((8, 2048), F32), pltpu.SemaphoreType.DMA((3,))],
             name="finish",
-        )(*(pltpu.with_memory_space_constraint(v, vmem) for v in (air, ocean, left, hot)), ocean_area.reshape(16, 128))
+        )(*(pltpu.with_memory_space_constraint(v, vmem) for v in (air, ocean, left, hot, area)))
         return air.reshape(air_shape), ocean.reshape(ocean_shape)
 
     both = ("face", "blk")

time: 47.8 us -> 47 us (0.983)
  Pallas kernels: 46.9 us -> 46.2 us
    pallas_call x1, Pallas kernels: 2.15 us -> 1.45 us  [body(): pl.pallas_call(finish_kernel, out_shape=(jax.ShapeDtypeStruct((768, 128),...]
where the time goes in v7:
time: 47 us; the launch traced here: 46.9 us
  Pallas kernels  46.2 us (98%)
  between operations  0.64 us (1%)
    pallas_call x1, Pallas kernels, body(): pl.pallas_call(lambda *refs: interval_kernel(n_face, n_blk, *refs), out_s...  44.8 us
    pallas_call x1, Pallas kernels, body(): pl.pallas_call(finish_kernel, out_shape=(jax.ShapeDtypeStruct((768, 128),...  1.45 us

profile of v7, /device:TPU:1, one launch (start us, length us, event | category | flops | bytes accessed | tf_op | source)
XLA Modules:
  0.0 46.9 jit_solution(3458646620365260700)
XLA Ops:
  0.6 44.8 %interval.1 = (f32[768,128]{1,0:T(8,128)S(1)}, f32[32,2048]{1,0:T(8,128)S(1)}, bf16[32,8192]{1,0:T(8,128)(2,1)S(1)}, bf16[128,8192]{1,0:T(8,128)(2,1)S(1)}, f32[16,128]{1,0:T(8,128)S(1)}) custom-call(f32[768,128]{1,0:T(8,128)} %bitcast.11, f32[512,128]{1,0:T(8,128)} %bitcast.12, f32[16,128]{1,0:T(8,128)} %refs_2_.1, f32[16,128]{1,0:T(8,128)} %refs_3_.1, ...), custom_call_target="tpu_custom_call" | custom-call | tf_op jit(solution)/shard_map/interval/pallas_call | solution.py:641
  45.4 1.4 %finish.1 = (f32[768,128]{1,0:T(8,128)}, f32[32,2048]{1,0:T(8,128)}) custom-call(f32[768,128]{1,0:T(8,128)S(1)} %get-tuple-element.9.air_ref, f32[32,2048]{1,0:T(8,128)S(1)} %get-tuple-element.10.ocean_ref, bf16[32,8192]{1,0:T(8,128)(2,1)S(1)} %get-tuple-element.11.left_ref, bf16[128,8192]{1,0:T(8,128)(2,1)S(1)} %get-tuple-element.12.hot_ref, ...), custom_call_target="tpu_custom_call" | custom-call | tf_op jit(solution)/shard_map/finish/pallas_call | solution.py:712
